TPU v7x, 32 devices: a whole 2x2x4 slice. The times are simulated.
32 devices in a mesh: dp: 8 (over z, core), tp: 4 (over y, x).
Axes of the slice: x: 2, y: 2, z: 4, core: 2. Of those that a mesh axis runs over, the one named last changes fastest.
Arguments:
- x_in: bfloat16 [8192, 2048], P(('dp', 'tp')), may hold values from -6 to 6
- norm_gain: float32 [2048], replicated, may hold values from 0.5 to 1.5
- w_z: bfloat16 [2048, 4096], P(None, 'tp'), may hold values from -0.125 to 0.125
- w_x: bfloat16 [2048, 4096], P(None, 'tp'), may hold values from -0.125 to 0.125
- w_b: bfloat16 [2048, 128], P(None, 'tp'), may hold values from -0.125 to 0.125
- w_c: bfloat16 [2048, 128], P(None, 'tp'), may hold values from -0.125 to 0.125
- w_dt: bfloat16 [2048, 64], P(None, 'tp'), may hold values from -0.125 to 0.125
- conv_w: float32 [4352, 4], replicated, may hold values from -3 to 3
- conv_b: float32 [4352], replicated, may hold values from -3 to 3
- dt_bias: float32 [64], replicated, may hold values from -6 to -2
- a_log: float32 [64], replicated, may hold values from -2.5 to 0.5
- d_skip: float32 [64], replicated, may hold values from 0.5 to 1.5
- gate_gain: float32 [4096], replicated, may hold values from 0.5 to 1.5
- w_out: bfloat16 [4096, 2048], P('tp'), may hold values from -0.09375 to 0.09375
- doc_lens: int32 [8, 8], P('dp'), may hold values from 1 to 512, 1024 in all within a row
- d_out: bfloat16 [8192, 2048], P(('dp', 'tp')), may hold values from -6 to 6
Outputs:
- block_out: bfloat16 [8192, 2048], P(('dp', 'tp'))
- grad_x: float32 [8192, 2048], P(('dp', 'tp'))
- grad_norm_gain: float32 [2048], replicated
- grad_w_z: float32 [2048, 4096], P('dp', 'tp')
- grad_w_x: float32 [2048, 4096], P('dp', 'tp')
- grad_w_b: float32 [2048, 128], P('dp', 'tp')
- grad_w_c: float32 [2048, 128], P('dp', 'tp')
- grad_w_dt: float32 [2048, 64], P('dp', 'tp')
- grad_conv_w: float32 [4352, 4], replicated
- grad_conv_b: float32 [4352], replicated
- grad_dt_bias: float32 [64], replicated
- grad_a_log: float32 [64], replicated
- grad_d_skip: float32 [64], replicated
- grad_gate_gain: float32 [4096], replicated
- grad_w_out: float32 [4096, 2048], P('tp', 'dp')
Inputs may be any that keep to these rules, and one draw needn't show every extreme that they name: `doc_lens`: each row gives, in order, the lengths of the 8 documents packed into one sequence of 1024 tokens; a row sums to 1024 and its longest document has exactly 512 tokens.
All inputs are finite; a program needn't handle non-finite values.
Results may differ from a plain program's by a relative error of at most 0.012.
Values may be sent and summed in bfloat16 or wider, within the bound.
A program may use at most 256 MiB of HBM per device.

v0:
```python
import jax
import jax.numpy as jnp
from jax import lax
from jax.sharding import PartitionSpec as P

EPSILON = 1e-05
HIGHEST = lax.Precision.HIGHEST


def entering_2(array, axis, combine, identity, reverse):
    count, index = (lax.axis_size(axis), lax.axis_index(axis))
    everything = jax.tree.map(lambda part: lax.all_gather(part, axis), array)
    start = jax.tree.map(
        lambda part, zero: jnp.broadcast_to(jnp.asarray(zero, part.dtype), part.shape),
        array,
        identity,
    )

    def lap(k, before):
        at = count - 1 - k if reverse else k
        reached = at > index if reverse else at < index
        new = combine(before, jax.tree.map(lambda part: part[at], everything))
        return jax.tree.map(lambda a, b: jnp.where(reached, a, b), new, before)

    return lax.fori_loop(0, count, lap, start)


def span_parts(log_decay, segments, segment_prev):
    cumulative = jnp.cumsum(log_decay, axis=0)
    inward = jnp.exp(cumulative) * (segments == segment_prev).astype(jnp.float32)[:, None]
    carried = jnp.exp(cumulative[-1]) * (segments[-1] == segment_prev).astype(jnp.float32)
    return (cumulative, inward, carried)


def span_pass(state, values, b_rows, c_rows, log_decay, steps_dt, segments, segment_prev):
    cumulative, inward, carried = span_parts(log_decay, segments, segment_prev)
    length = segments.shape[0]
    order = jnp.arange(length, dtype=jnp.int32)
    same = (segments[:, None] == segments[None, :]) & (order[:, None] >= order[None, :])
    spread = cumulative[:, None, :] - cumulative[None, :, :]
    decays = jnp.exp(jnp.where(same[:, :, None], spread, -1e30))
    scores = jnp.dot(c_rows, b_rows.T, precision=HIGHEST)
    mixing = decays * scores[:, :, None] * steps_dt[None, :, :]
    output = jnp.einsum("tsh,shp->thp", mixing, values, precision=HIGHEST)
    output = (
        output + jnp.einsum("tn,hpn->thp", c_rows, state, precision=HIGHEST) * inward[:, :, None]
    )
    tail_same = segments == segments[-1]
    tail = (
        jnp.exp(jnp.where(tail_same[:, None], cumulative[-1][None, :] - cumulative, -1e30))
        * steps_dt
    )
    weighted = tail[:, :, None] * values
    state_out = carried[:, None, None] * state + jnp.einsum(
        "shp,sn->hpn", weighted, b_rows, precision=HIGHEST
    )
    return (output, state_out, carried)


def in_norm(values, gain):
    return (
        values
        * lax.rsqrt(jnp.mean(values * values, axis=-1, keepdims=True) + EPSILON)
        * gain[None, :]
    )


def combine(earlier, later):
    return (earlier[0] * later[0], later[0][:, None, None] * earlier[1] + later[1])


def body(
    x_in,
    norm_gain,
    w_z,
    w_x,
    w_b,
    w_c,
    w_dt,
    conv_w,
    conv_b,
    dt_bias,
    a_log,
    d_skip,
    gate_gain,
    w_out,
    doc_lens,
    d_out,
):
    tp_count = lax.axis_size("tp")
    tp_rank = lax.axis_index("tp")
    dev_rows = x_in.shape[0]
    group_rows = dev_rows * tp_count
    head_count = dt_bias.shape[0]
    inner_width = gate_gain.shape[0]
    head_size = inner_width // head_count
    state_size = (conv_w.shape[0] - inner_width) // 2
    rim_rows = conv_w.shape[1] - 1
    col_widths = [w_z.shape[1], w_x.shape[1], w_b.shape[1], w_c.shape[1], w_dt.shape[1]]
    col_edges = [0]
    for col_width in col_widths:
        col_edges.append(col_edges[-1] + col_width)
    total_cols = col_edges[-1]
    contract_first = (((0,), (0,)), ((), ()))
    contract_last = (((1,), (1,)), ((), ()))
    lengths = doc_lens[0]
    doc_starts = jnp.cumsum(lengths) - lengths
    positions = tp_rank * dev_rows - rim_rows + jnp.arange(dev_rows + rim_rows, dtype=jnp.int32)
    seg_ext = jnp.sum((positions[:, None] >= doc_starts[None, :]).astype(jnp.int32), axis=1)
    seg_own = seg_ext[rim_rows:]
    seg_before = [seg_ext[rim_rows - 1]]
    x_float = x_in.astype(jnp.float32)
    normed = in_norm(x_float, norm_gain).astype(jnp.bfloat16)
    w_joined = jnp.concatenate([w_z, w_x, w_b, w_c, w_dt], axis=1)
    gathered = lax.all_gather(normed, "tp", axis=0, tiled=True)
    projected = jnp.dot(gathered, w_joined, preferred_element_type=jnp.float32).astype(jnp.bfloat16)
    padded = jnp.concatenate([jnp.zeros((rim_rows, total_cols), jnp.bfloat16), projected], axis=0)
    rims = padded[:group_rows].reshape(tp_count, dev_rows, total_cols)[:, :rim_rows]
    blocks = jnp.concatenate([rims, projected.reshape(tp_count, dev_rows, total_cols)], axis=1)
    arrived = lax.all_to_all(blocks, "tp", split_axis=0, concat_axis=2, tiled=True).reshape(
        dev_rows + rim_rows, tp_count, total_cols
    )

    def columns(source, which):
        return source[:, :, col_edges[which] : col_edges[which + 1]].reshape(source.shape[0], -1)

    gate_in = columns(arrived[rim_rows:], 0).astype(jnp.float32)
    conv_in = jnp.concatenate(
        [columns(arrived, 1), columns(arrived, 2), columns(arrived, 3)], axis=1
    ).astype(jnp.float32)
    dt_in = columns(arrived[rim_rows:], 4).astype(jnp.float32)

    def prepare(conv_in, dt_in, conv_w, conv_b, dt_bias, a_log):
        summed = jnp.zeros((dev_rows, conv_in.shape[1]), jnp.float32) + conv_b[None, :]
        for kernel_tap in range(conv_w.shape[1]):
            match = (seg_ext[kernel_tap : kernel_tap + dev_rows] == seg_own).astype(jnp.float32)
            summed = (
                summed
                + conv_w[:, kernel_tap][None, :]
                * conv_in[kernel_tap : kernel_tap + dev_rows]
                * match[:, None]
            )
        active = jax.nn.silu(summed)
        values = active[:, :inner_width].reshape(dev_rows, head_count, head_size)
        b_rows = active[:, inner_width : inner_width + state_size]
        c_rows = active[:, inner_width + state_size :]
        steps_dt = jax.nn.softplus(dt_in + dt_bias[None, :])
        log_decay = -steps_dt * jnp.exp(a_log)[None, :]
        return (values, b_rows, c_rows, log_decay, steps_dt)

    prepared, prepare_back = jax.vjp(prepare, conv_in, dt_in, conv_w, conv_b, dt_bias, a_log)
    values, b_rows, c_rows, log_decay, steps_dt = prepared

    def ssd_local(values, b_rows, c_rows, log_decay, steps_dt):
        state = jnp.zeros((head_count, head_size, state_size), jnp.float32)
        carried_all = jnp.ones((head_count,), jnp.float32)
        output, state, carried = span_pass(
            state, values, b_rows, c_rows, log_decay, steps_dt, seg_own, seg_before[0]
        )
        outputs = [output]
        carried_all = carried_all * carried
        return (jnp.concatenate(outputs, axis=0), carried_all, state)

    def entering(state_in, c_rows, log_decay):
        decay = jnp.ones((head_count,), jnp.float32)
        cumulative, inward, carried = span_parts(log_decay, seg_own, seg_before[0])
        reached = jnp.einsum(
            "tn,hpn->thp", c_rows, decay[:, None, None] * state_in, precision=HIGHEST
        )
        outputs = [reached * inward[:, :, None]]
        return jnp.concatenate(outputs, axis=0)

    identity = (
        jnp.ones((head_count,), jnp.float32),
        jnp.zeros((head_count, head_size, state_size), jnp.float32),
    )
    local_parts, ssd_back = jax.vjp(ssd_local, values, b_rows, c_rows, log_decay, steps_dt)
    local_out, carried_dev, state_dev = local_parts
    chained = entering_2((carried_dev, state_dev), "tp", combine, identity, False)
    state_in = chained[1]
    extra_out, entering_back = jax.vjp(entering, state_in, c_rows, log_decay)
    ssd_out = local_out + extra_out

    def gated(ssd_out, values, gate_in, d_skip, gate_gain):
        mixed_heads = ssd_out + d_skip[None, :, None] * values
        flat = mixed_heads.reshape(dev_rows, inner_width)
        gated_rows = flat * jax.nn.silu(gate_in)
        scale = lax.rsqrt(jnp.mean(gated_rows * gated_rows, axis=-1, keepdims=True) + EPSILON)
        return gated_rows * scale * gate_gain[None, :]

    normal_out, gated_back = jax.vjp(gated, ssd_out, values, gate_in, d_skip, gate_gain)
    rounded = normal_out.astype(jnp.bfloat16)
    by_heads = lax.all_to_all(rounded, "tp", split_axis=1, concat_axis=0, tiled=True)
    branch_out = lax.psum_scatter(
        jnp.dot(by_heads, w_out, preferred_element_type=jnp.float32),
        "tp",
        scatter_dimension=0,
        tiled=True,
    )
    block_out = (x_float + branch_out).astype(jnp.bfloat16)
    grad_gathered = lax.all_gather(d_out, "tp", axis=0, tiled=True)
    grad_heads = lax.dot_general(
        grad_gathered, w_out, contract_last, preferred_element_type=jnp.float32
    ).astype(jnp.bfloat16)
    grad_normal = lax.all_to_all(grad_heads, "tp", split_axis=0, concat_axis=1, tiled=True)
    grad_ssd, grad_values_a, grad_gate_in, grad_skip, grad_gate_gain = gated_back(
        grad_normal.astype(jnp.float32)
    )
    grad_state_in, grad_c_a, grad_decay_a = entering_back(grad_ssd)
    chained_back = entering_2((carried_dev, grad_state_in), "tp", combine, identity, True)
    grad_state_dev = chained_back[1]
    grad_carried = jnp.sum(grad_state_dev * state_in, axis=(1, 2))
    grad_values_b, grad_b, grad_c_b, grad_decay_b, grad_dt = ssd_back(
        (grad_ssd, grad_carried, grad_state_dev)
    )
    grad_conv_in, grad_dt_in, grad_conv_w, grad_conv_b, grad_dt_bias, grad_a_log = prepare_back(
        (
            grad_values_a + grad_values_b,
            grad_b,
            grad_c_a + grad_c_b,
            grad_decay_a + grad_decay_b,
            grad_dt,
        )
    )

    def split_heads(array):
        return array.reshape(array.shape[0], tp_count, -1)

    grad_gate_full = jnp.concatenate(
        [jnp.zeros((rim_rows, inner_width), jnp.float32), grad_gate_in], axis=0
    )
    grad_dt_full = jnp.concatenate(
        [jnp.zeros((rim_rows, head_count), jnp.float32), grad_dt_in], axis=0
    )
    pieces = [
        split_heads(grad_gate_full),
        split_heads(grad_conv_in[:, :inner_width]),
        split_heads(grad_conv_in[:, inner_width : inner_width + state_size]),
        split_heads(grad_conv_in[:, inner_width + state_size :]),
        split_heads(grad_dt_full),
    ]
    outgoing = jnp.concatenate(pieces, axis=2).reshape(
        1, dev_rows + rim_rows, tp_count * total_cols
    )
    returned = lax.all_to_all(outgoing, "tp", split_axis=2, concat_axis=0, tiled=True)
    main_rows = returned[:, rim_rows:]
    main_rows = main_rows.at[:-1, dev_rows - rim_rows :].add(returned[1:, :rim_rows])
    grad_projected = main_rows.reshape(group_rows, total_cols).astype(jnp.bfloat16)
    grad_normed = lax.psum_scatter(
        lax.dot_general(
            grad_projected, w_joined, contract_last, preferred_element_type=jnp.float32
        ),
        "tp",
        scatter_dimension=0,
        tiled=True,
    )
    _, norm_back = jax.vjp(in_norm, x_float, norm_gain)
    grad_x_norm, grad_norm_gain = norm_back(grad_normed)
    grad_x = d_out.astype(jnp.float32) + grad_x_norm
    in_part = lax.dot_general(
        gathered, grad_projected, contract_first, preferred_element_type=jnp.float32
    )
    weight_grads = lax.psum_scatter(
        jnp.concatenate(
            [
                in_part,
                lax.dot_general(
                    grad_gathered, by_heads, contract_first, preferred_element_type=jnp.float32
                ),
            ],
            axis=1,
        ),
        "dp",
        scatter_dimension=0,
        tiled=True,
    )
    grad_w_z = weight_grads[:, col_edges[0] : col_edges[1]]
    grad_w_x = weight_grads[:, col_edges[1] : col_edges[2]]
    grad_w_b = weight_grads[:, col_edges[2] : col_edges[3]]
    grad_w_c = weight_grads[:, col_edges[3] : col_edges[4]]
    grad_w_dt = weight_grads[:, col_edges[4] : col_edges[5]]
    grad_w_out = weight_grads[:, total_cols:].T
    summed_small = lax.psum(
        (
            grad_norm_gain,
            grad_conv_w,
            grad_conv_b,
            grad_dt_bias,
            grad_a_log,
            grad_skip,
            grad_gate_gain,
        ),
        ("dp", "tp"),
    )
    return (
        block_out,
        grad_x,
        summed_small[0],
        grad_w_z,
        grad_w_x,
        grad_w_b,
        grad_w_c,
        grad_w_dt,
        summed_small[1],
        summed_small[2],
        summed_small[3],
        summed_small[4],
        summed_small[5],
        summed_small[6],
        grad_w_out,
    )


def solution(mesh):
    placed = (
        P(("dp", "tp"), None),
        P(),
        P(None, "tp"),
        P(None, "tp"),
        P(None, "tp"),
        P(None, "tp"),
        P(None, "tp"),
        P(),
        P(),
        P(),
        P(),
        P(),
        P(),
        P("tp", None),
        P("dp", None),
        P(("dp", "tp"), None),
    )
    return jax.shard_map(
        body,
        mesh=mesh,
        in_specs=placed,
        out_specs=(
            P(("dp", "tp"), None),
            P(("dp", "tp"), None),
            P(),
            P("dp", "tp"),
            P("dp", "tp"),
            P("dp", "tp"),
            P("dp", "tp"),
            P("dp", "tp"),
            P(),
            P(),
            P(),
            P(),
            P(),
            P(),
            P("tp", "dp"),
        ),
        check_vma=False,
    )
```

profile of v0, /device:TPU:0, one launch (start us, length us, event | category | flops | bytes accessed | tf_op | source)
XLA Modules:
  0.0 1442.2 jit_solution(17318158812077434221)
XLA Ops:
  12.3 14.3 concatenate.29
  26.6 40.4 %all-gather.8.cloned.1.call-done = bf16[1024,2048]{1,0:T(8,128)(2,1)} async-done(((bf16[256,2048]{1,0:T(8,128)(2,1)}), bf16[1024,2048]{1,0:T(8,128)(2,1)}) %all-gather.8.cloned.1.call-update) | async-done | bytes 4194320 | tf_op jit(solution)/shard_map/all_gather | solution.py:115
  67.0 13.6 convolution_convert_fusion
  82.7 4.6 pad_slice_fusion
  87.3 6.4 copy.204
  93.7 6.4 copy.203
  101.0 5.6 pad_maximum_fusion.1
  106.6 5.0 all-to-all-start
  117.7 63.9 %all-to-all-done = bf16[4,259,2128]{2,1,0:T(8,128)(2,1)} async-done(((bf16[4,259,2128]{2,1,0:T(8,128)(2,1)}), bf16[4,259,2128]{2,1,0:T(8,128)(2,1)}, u32[]{:S(2)}, u32[]{:S(2)}) %all-to-all-start) | async-done | bytes 4409248 | tf_op jit(solution)/shard_map/all_to_all | solution.py:120
  181.5 8.2 copy.176
  189.7 5.1 slice_bitcast_fusion
  206.1 4.9 fusion.25
  215.6 6.0 copy.180
  222.1 7.0 fusion.78
  229.2 8.0 convolution_convert_fusion.1
  239.8 4.4 all-to-all-start.2
  244.5 41.5 %all-to-all-done.2 = bf16[4,256,1024]{1,2,0:T(8,128)(2,1)} async-done(((bf16[4,256,1024]{1,2,0:T(8,128)(2,1)}), bf16[4,256,1024]{1,2,0:T(8,128)(2,1)}, u32[]{:S(2)}, u32[]{:S(2)}) %all-to-all-start.2) | async-done | bytes 2097184 | tf_op jit(solution)/shard_map/all_to_all | solution.py:205
  286.0 4.0 convert_element_type.132
  290.0 7.9 all-gather.2
  299.3 6.2 fusion.92
  309.3 30.0 %all-gather.12.cloned.1.call-done = f32[256,64,128]{2,1,0:T(8,128)} async-done(((f32[64,64,128]{2,1,0:T(8,128)}), f32[256,64,128]{2,1,0:T(8,128)}) %all-gather.12.cloned.1.call-update) | async-done | bytes 8388624 | tf_op jit(solution)/shard_map/all_gather | solution.py:12
  339.4 8.5 while.31
  347.8 4.5 fusion.100
  352.4 23.6 %multiply_reduce_fusion.11 = (f32[256]{0:T(256)S(1)}, f32[256,64,64]{0,2,1:T(8,128)S(1)}, f32[256,64,64]{0,2,1:T(8,128)}) fusion(f32[256,64,64]{0,2,1:T(8,128)} %bitcast.311, f32[256,64,64]{0,2,1:T(8,128)S(1)} %bitcast.299, f32[64]{0:T(128)S(1)} %copy-done.73, f32[256,64,64]{0,2,1:T(8,128)S(1)} %fusion.100, f32[256,64,64]{0,2,1:T(8,128)} %fusion.92, ...), kind=kOutput, calls=%fused_computation.87 | convolution fusion | flops 3251633920 | bytes 25691392 | tf_op jit(solution)/shard_map/jvp(tsh,shp->thp)/dot_general | solution.py:44
  378.2 5.8 multiply_reduce_fusion.6
  386.0 5.6 fusion.53
  394.4 5.0 fusion.28
  399.4 4.5 concatenate.33
  403.9 7.6 copy.193
  411.5 9.0 fusion.84
  420.6 6.7 fusion.81
  427.3 26.2 %fusion.10 = (f32[256,64]{0,1:T(8,128)S(1)}, f32[256,64]{0,1:T(8,128)S(1)}, f32[256,64]{0,1:T(8,128)}, f32[256,256]{1,0:T(8,128)S(1)}) fusion(f32[256,64]{0,1:T(8,128)S(1)} %copy-done.43, f32[256,256]{1,0:T(8,128)S(1)} %copy-done.23, f32[256,64]{0,1:T(8,128)S(1)} %bitcast_bitcast_fusion.1, pred[256,256]{1,0:T(8,128)(4,1)S(1)} %fusion.95, ...), kind=kOutput, calls=%fused_computation.18 | convolution fusion | flops 3275636736 | bytes 9306112 | tf_op jit(solution)/shard_map/transpose(jvp(tsh,shp->thp))/dot_general | solution.py:44
  454.7 24.6 %all-gather.14.cloned.1.call-done = f32[256,64,128]{2,1,0:T(8,128)} async-done(((f32[64,64,128]{2,1,0:T(8,128)}), f32[256,64,128]{2,1,0:T(8,128)}) %all-gather.14.cloned.1.call-update) | async-done | bytes 8388624 | tf_op jit(solution)/shard_map/all_gather | solution.py:12
  479.4 14.9 %while.32 = (s32[]{:T(128)}, f32[64,64,128]{2,1,0:T(8,128)}, s32[]{:T(128)}, f32[4,64]{1,0:T(4,128)S(1)}, f32[4,64,64,128]{3,2,1,0:T(8,128)}, /*index=5*/s32[]{:T(128)}, s32[]{:T(128)}, s32[]{:T(128)}, s32[]{:T(128)}) while((s32[]{:T(128)}, f32[64,64,128]{2,1,0:T(8,128)}, s32[]{:T(128)}, f32[4,64]{1,0:T(4,128)S(1)}, ...), condition=%wide.region_12.13_spmd.clone, body=%wide.region_11.12_spmd.clone.sunk | while | flops 2097160 | bytes 6292391 | solution.py:25
  494.3 9.8 fusion.87
  504.1 4.5 multiply_reduce_fusion.9
  511.1 15.7 %fusion.31 = f32[256,64,64]{0,2,1:T(8,128)} fusion(f32[256,64,64]{0,2,1:T(8,128)S(1)} %get-tuple-element.469, f32[256,64,64]{0,2,1:T(8,128)S(1)} %copy-done.7, f32[64]{0:T(128)S(1)} %copy-done.73, f32[256,64]{0,1:T(8,128)S(1)} %get-tuple-element.456, f32[256,64]{0,1:T(8,128)S(1)} %copy-done.43, f32[256,256]{1,0:T(8,128)S(1)} %copy-done.24, ...), kind=kOutput, calls=%fused_computation.58 | convolution fusion | flops 3242196992 | bytes 13107456 | tf_op jit(solution)/shard_map/transpose(jvp(tsh,shp->thp))/dot_general | solution.py:44
  526.8 5.8 copy.185
  532.6 12.2 multiply_reduce_fusion.4
  549.9 7.2 pad_add_fusion
  562.0 4.7 slice.230
  566.7 6.1 reshape.445
  572.8 15.8 %concatenate.35 = f32[259,4,2128]{2,1,0:T(4,128)} concatenate(f32[259,4,1024]{2,1,0:T(4,128)} %copy.193, f32[259,4,1024]{2,1,0:T(4,128)} %reshape.445, f32[259,4,32]{2,1,0:T(4,128)S(1)} %copy.194, f32[259,4,32]{2,1,0:T(4,128)S(1)} %copy.195, f32[259,4,16]{2,1,0:T(4,128)S(1)} %copy.196), dimensions={2} | concatenate | bytes 17636864 | tf_op jit(solution)/shard_map/concatenate | solution.py:242
  588.6 11.4 reshape.454
  600.0 27.3 %copy.197 = f32[1,259,8512]{1,0,2:T(1,128)} copy(f32[1,259,8512]{2,1,0:T(8,128)} %reshape.454) | data formatting | bytes 17636864 | tf_op jit(solution)/shard_map/reshape | solution.py:242
  627.3 6.5 all-to-all-start.3
  635.1 141.5 %all-to-all-done.3 = f32[1,259,8512]{1,0,2:T(1,128)} async-done(((f32[1,259,8512]{1,0,2:T(1,128)}), f32[1,259,8512]{1,0,2:T(1,128)}, u32[]{:S(2)}, u32[]{:S(2)}) %all-to-all-start.3) | async-done | bytes 8818464 | tf_op jit(solution)/shard_map/all_to_all | solution.py:245
  776.6 12.1 copy.207
  788.7 7.0 slice.233
  799.1 4.8 add_select_fusion
  803.9 22.9 %scatter-add.4 = f32[4,256,2128]{1,2,0:T(8,128)} dynamic-update-slice(f32[4,256,2128]{1,2,0:T(8,128)} %copy-done.8, f32[3,3,2128]{1,2,0:T(8,128)S(1)} %add_select_fusion, s32[]{:T(128)} %bitcast.52, s32[]{:T(128)} %bitcast.53, s32[]{:T(128)} %constant.140.clone.1) | dynamic-update-slice | bytes 153220 | tf_op jit(solution)/shard_map/scatter-add | solution.py:247
  826.8 5.9 convert_element_type.125
  832.7 6.4 copy.200
  839.1 15.7 %fusion.148 = f32[1024,2048]{1,0:T(8,128)} fusion(bf16[1024,2128]{1,0:T(8,128)(2,1)} %bitcast.319, bf16[2048,2128]{1,0:T(8,128)(2,1)} %concatenate.29), kind=kOutput, calls=%fused_computation.237 | convolution fusion | flops 8925478912 | bytes 21463040 | tf_op jit(solution)/shard_map/dot_general | solution.py:250
  859.2 50.7 %all_to_all.62 = bf16[256,4,1024]{0,2,1:T(8,128)(2,1)S(1)} all-to-all(bf16[256,4,1024]{0,2,1:T(8,128)(2,1)S(1)} %fusion.48), channel_id=1, replica_groups=mesh['dp'=8,'tp'=4] {'tp'}, dimensions={1} | all-to-all | bytes 4194304 | tf_op jit(solution)/shard_map/all_to_all | solution.py:193
  912.3 10.8 fusion.147
  924.7 9.0 convolution_bitcast_fusion
  933.7 12.9 fusion.149
  946.5 16.0 %pad_maximum_fusion = f32[2048,3152]{0,1:T(8,128)} fusion(f32[2048,1024]{0,1:T(8,128)} %convolution_bitcast_fusion, f32[2048,2128]{0,1:T(8,128)S(1)} %fusion.149), kind=kLoop, calls=%fused_computation.6 | loop fusion | flops 6455296 | bytes 51642368 | tf_op jit(solution)/shard_map/concatenate | solution.py:264
  966.8 41.3 %all-reduce.16 = (f32[2048]{0:T(1024)}, f32[4352]{0:T(1024)}, f32[64]{0:T(128)}, f32[64]{0:T(128)}, f32[64]{0:T(128)}, /*index=5*/f32[4096]{0:T(1024)}) all-reduce(f32[2048]{0:T(1024)S(1)} %get-tuple-element.395, f32[4352]{0:T(1024)S(1)} %copy-done.32, f32[64]{0:T(128)S(1)} %get-tuple-element.431, ...), channel_id=1, replica_groups=mesh['dp'=8,'tp'=4] {'dp','tp'}, use_global_device_ids=true, to_apply=%region_30.31 | all-reduce | flops 10688 | bytes 85504 | tf_op jit(solution)/shard_map/psum | solution.py:283
  1008.1 46.6 %reduce-scatter.4.cloned.1.call-done = f32[256,2048]{1,0:T(8,128)} async-done(((f32[1024,2048]{1,0:T(8,128)}), f32[256,2048]{1,0:T(8,128)}) %reduce-scatter.4.cloned.1.call-update) | async-done | bytes 2097168 | tf_op jit(solution)/shard_map/reduce_scatter | solution.py:194
  1054.7 4.3 fusion.65
  1059.0 251.4 %reduce-scatter.8.cloned.1.call-done = f32[256,3152]{0,1:T(8,128)} async-done(((f32[2048,3152]{0,1:T(8,128)}), f32[256,3152]{0,1:T(8,128)}) %reduce-scatter.8.cloned.1.call-update) | async-done | bytes 3227664 | tf_op jit(solution)/shard_map/reduce_scatter | solution.py:263
  1318.7 114.9 %all-reduce.19.cloned.1.call-done = f32[4352,4]{0,1:T(4,128)} async-done(((f32[4352,4]{0,1:T(4,128)}), f32[4352,4]{0,1:T(4,128)}) %all-reduce.19.cloned.1.call-update) | async-done | bytes 69648 | tf_op jit(solution)/shard_map/psum | solution.py:283
  (277 shorter events, 107.7 us)
Async XLA Ops:
  7.2 4.2 copy-start.30
  7.2 4.5 copy-start.31
  7.2 4.8 copy-start.39
  7.2 59.8 %all-gather.8.cloned.1.call-start = ((), (), s32[]{:S(2)}) async-start(), calls=%async_computation.7 | async-start | bytes 5242880 | tf_op jit(solution)/shard_map/all_gather | solution.py:115
  8.8 2.6 copy-start.66
  8.9 2.6 copy-start.57
  106.6 6.1 copy-start.74
  106.6 6.1 copy-start.72
  106.6 8.3 copy-start.38
  106.6 74.9 %all-to-all-start = ((bf16[4,259,2128]{2,1,0:T(8,128)(2,1)}), bf16[4,259,2128]{2,1,0:T(8,128)(2,1)}, u32[]{:S(2)}, u32[]{:S(2)}) async-start(bf16[4,259,2128]{2,1,0:T(8,128)(2,1)} %pad_maximum_fusion.1), calls=%async_computation | async-start | bytes 9191424 | tf_op jit(solution)/shard_map/all_to_all | solution.py:120
  111.7 117.5 %all-gather.10.cloned.1.call-start = ((), (), s32[]{:S(2)}) async-start(), calls=%async_computation.9 | async-start | bytes 5242880 | tf_op jit(solution)/shard_map/all_gather | solution.py:201
  112.4 226.9 %all-gather.12.cloned.1.call-start = ((), (), s32[]{:S(2)}) async-start(), calls=%async_computation.13 | async-start | bytes 10485760 | tf_op jit(solution)/shard_map/all_gather | solution.py:12
  112.7 84.2 %copy-start.68 = (f32[64]{0:T(128)}, f32[64]{0:T(128)S(1)}, u32[]{:S(2)}) copy-start(f32[64]{0:T(128)S(1)} %exp.58) | copy-start | bytes 772
  113.0 76.7 %copy-start.45 = (s32[259]{0:T(512)}, s32[259]{0:T(512)S(1)}, u32[]{:S(2)}) copy-start(s32[259]{0:T(512)S(1)} %convert_reduce_fusion) | copy-start | bytes 3112
  189.7 7.2 copy-start.59
  196.9 25.0 %copy-start.20 = (bf16[256,4,16]{0,2,1:T(8,128)(2,1)}, bf16[256,4,16]{0,2,1:T(8,128)(2,1)S(1)}, u32[]{:S(2)}) copy-start(bf16[256,4,16]{0,2,1:T(8,128)(2,1)S(1)} %slice.224) | copy-start | bytes 98308
  206.0 4.9 copy-start
  215.6 6.4 copy-start.50
  215.6 6.4 copy-start.60
  215.6 6.4 copy-start.64
  221.9 7.2 copy-start.62
  222.1 130.2 %copy-start.42 = (f32[256,64]{0,1:T(8,128)}, f32[256,64]{0,1:T(8,128)S(1)}, u32[]{:S(2)}) copy-start(f32[256,64]{0,1:T(8,128)S(1)} %get-tuple-element.457) | copy-start | bytes 196612
  237.2 7.1 copy-start.46
  237.2 7.2 copy-start.27
  239.8 46.3 %all-to-all-start.2 = ((bf16[4,256,1024]{1,2,0:T(8,128)(2,1)}), bf16[4,256,1024]{1,2,0:T(8,128)(2,1)}, u32[]{:S(2)}, u32[]{:S(2)}) async-start(bf16[4,256,1024]{1,2,0:T(8,128)(2,1)} %copy.184), calls=%async_computation.3 | async-start | bytes 4194304 | tf_op jit(solution)/shard_map/all_to_all | solution.py:205
  244.2 235.2 %all-gather.14.cloned.1.call-start = ((), (), s32[]{:S(2)}) async-start(), calls=%async_computation.14 | async-start | bytes 10485760 | tf_op jit(solution)/shard_map/all_gather | solution.py:12
  244.5 182.7 %copy-start.40 = (pred[256,256]{1,0:T(8,128)(4,1)}, pred[256,256]{1,0:T(8,128)(4,1)S(1)}, u32[]{:S(2)}) copy-start(pred[256,256]{1,0:T(8,128)(4,1)S(1)} %fusion.95) | copy-start | bytes 196612
  299.2 53.1 %copy-start.22 = (f32[256,256]{1,0:T(8,128)}, f32[256,256]{1,0:T(8,128)S(1)}, u32[]{:S(2)}) copy-start(f32[256,256]{1,0:T(8,128)S(1)} %fusion.106) | copy-start | bytes 786436
  347.8 4.5 copy-start.2
  347.8 4.5 copy-start.73
  352.3 23.7 %copy-start.16 = (f32[256,64,64]{0,2,1:T(8,128)}, f32[256,64,64]{0,2,1:T(8,128)S(1)}, u32[]{:S(2)}) copy-start(f32[256,64,64]{0,2,1:T(8,128)S(1)} %fusion.100) | copy-start | bytes 12582916
  352.4 23.6 %copy-start.11 = (f32[4,256,1024]{1,2,0:T(8,128)S(1)}, f32[4,256,1024]{1,2,0:T(8,128)}, u32[]{:S(2)}) copy-start(f32[4,256,1024]{1,2,0:T(8,128)} %convert_element_type.132) | copy-start | bytes 12582916
  376.0 18.4 %copy-start.47 = (f32[256]{0:T(256)}, f32[256]{0:T(256)S(1)}, u32[]{:S(2)}) copy-start(f32[256]{0:T(256)S(1)} %fusion.132) | copy-start | bytes 3076
  376.0 2.2 copy-start.12
  411.5 9.0 copy-start.6
  420.5 6.7 copy-start.3
  420.6 6.7 copy-start.23
  420.6 6.7 copy-start.43
  494.3 9.8 copy-start.1
  494.3 9.8 copy-start.4
  508.6 2.5 copy-start.7
  508.6 2.5 copy-start.24
  508.6 2.5 copy-start.41
  526.8 5.8 copy-start.52
  526.8 5.8 copy-start.54
  526.8 5.8 copy-start.56
  546.2 3.4 copy-start.10
  549.8 7.2 copy-start.21
  549.8 7.2 copy-start.61
  549.8 7.2 copy-start.63
  549.8 7.2 copy-start.65
  549.9 10.6 copy-start.44
  549.9 10.6 copy-start.69
  627.3 7.1 copy-start.71
  627.3 149.3 %all-to-all-start.3 = ((f32[1,259,8512]{1,0,2:T(1,128)}), f32[1,259,8512]{1,0,2:T(1,128)}, u32[]{:S(2)}, u32[]{:S(2)}) async-start(f32[1,259,8512]{1,0,2:T(1,128)} %copy.197), calls=%async_computation.4 | async-start | bytes 26148864 | tf_op jit(solution)/shard_map/all_to_all | solution.py:245
  633.8 330.5 %reduce-scatter.6.cloned.1.call-start = ((), (), s32[]{:S(2)}) async-start(), calls=%async_computation.10 | async-start | bytes 10485760 | tf_op jit(solution)/shard_map/reduce_scatter | solution.py:249
  795.7 3.4 copy-start.8
  854.9 199.8 %reduce-scatter.4.cloned.1.call-start = ((), (), s32[]{:S(2)}) async-start(), calls=%async_computation.8 | async-start | bytes 10485760 | tf_op jit(solution)/shard_map/reduce_scatter | solution.py:194
  923.1 387.3 %reduce-scatter.8.cloned.1.call-start = ((), (), s32[]{:S(2)}) async-start(), calls=%async_computation.11 | async-start | bytes 29048832 | tf_op jit(solution)/shard_map/reduce_scatter | solution.py:263
  962.6 4.1 copy-start.67
  962.6 4.1 copy-start.32
  962.6 4.1 copy-start.70
  962.7 471.0 %all-reduce.19.cloned.1.call-start = ((), (), s32[]{:S(2)}) async-start(), calls=%async_computation.12 | async-start | bytes 139264 | tf_op jit(solution)/shard_map/psum | solution.py:283
  964.3 90.4 %copy-start.18 = (f32[256,2048]{1,0:T(8,128)S(1)}, f32[256,2048]{1,0:T(8,128)}, u32[]{:S(2)}) copy-start(f32[256,2048]{1,0:T(8,128)} %reduce-scatter.6.cloned.1.call-done) | copy-start | bytes 6291460
  (23 other events, 35.9 us)
Sparse Core Ops, SparseCore 0:
  11.5 55.3 all-gather.7
  114.4 83.1 all-gather.9
  229.2 110.0 all-gather.11
  391.7 87.6 all-gather.13
  855.0 108.8 reduce-scatter.5
  967.1 87.4 reduce-scatter.3
  1057.0 253.2 reduce-scatter.7
  1317.4 116.1 all-reduce.18
where the time goes:
time: 1460 us; the launch traced here: 1440 us
  waiting for transfers between devices  756 us (52%)
  local copies, waits for them, and re-layouts  230 us (16%)
  matrix products  193 us (13%)
  other arithmetic  130 us (9%)
  blocking collectives  99.9 us (7%)
  between operations  16.9 us (1%)
  starting transfers between devices  16.5 us (1%)
    reduce_scatter x1, waiting for transfers between devices, body(): lax.psum_scatter(jnp.concatenate([in_part, lax.dot_general(grad_gathered,...  251 us
    all_to_all x1, waiting for transfers between devices, body(): lax.all_to_all(outgoing, 'tp', split_axis=2, concat_axis=0, tiled=True)  141 us
    psum x1, waiting for transfers between devices, body(): lax.psum((grad_norm_gain, grad_conv_w, grad_conv_b, grad_dt_bias, grad_a_...  115 us
    dot_general x3, matrix products, span_pass(): output = jnp.einsum('tsh,shp->thp', mixing, values, precision=HIGHEST)  65.4 us
    all_to_all x1, waiting for transfers between devices, body(): lax.all_to_all(blocks, 'tp', split_axis=0, concat_axis=2, tiled=True)  63.9 us
    all_gather x2, waiting for transfers between devices, entering_2(): everything = jax.tree.map(lambda part: lax.all_gather(part, axis), array)  54.7 us
    all_to_all x1, blocking collectives, body(): lax.all_to_all(rounded, 'tp', split_axis=1, concat_axis=0, tiled=True)  50.7 us
    reduce_scatter x1, waiting for transfers between devices, body(): lax.psum_scatter(jnp.dot(by_heads, w_out, preferred_element_type=jnp.floa...  46.6 us
  transfers between devices with their start and end apart: 11, of which 9 were waited for; matrix products, arithmetic and copies ran while one was open for 15% of the time, Pallas kernels for 0%

commit v1 on v0

v1 whole, which is shorter than its diff:
```python
import functools

import jax
import jax.numpy as jnp
from jax import lax
from jax.experimental import pallas as pl
from jax.experimental.pallas import tpu as pltpu
from jax.sharding import PartitionSpec as P

EPSILON = 1e-05
HIGHEST = lax.Precision.HIGHEST
F32 = jnp.float32
BF16 = jnp.bfloat16
CHUNK = 128
LANES = 128
CONTRACT_FIRST = (((0,), (0,)), ((), ()))
CONTRACT_LAST = (((1,), (1,)), ((), ()))


def dot(a, b, dims=(((1,), (0,)), ((), ()))):
    return lax.dot_general(a, b, dims, preferred_element_type=F32)


def two_parts(v):
    high = v.astype(BF16)
    return jnp.concatenate([high, (v - high.astype(F32)).astype(BF16)], axis=1)


def prepare_chunk(width, x_ref, bc_ref, dt_ref, halo_x_ref, halo_bc_ref, pos_ref, prm_ref, head_ref, expand_ref, ext):
    rows = x_ref.shape[0]
    ext[8:, :width] = x_ref[...].astype(F32)
    ext[8:, width:] = bc_ref[...].astype(F32)
    ext[:8, :width] = halo_x_ref[...].astype(F32)[8:, :]
    ext[:8, width:] = halo_bc_ref[...].astype(F32)[8:, :]
    pos = pos_ref[...]
    pre = prm_ref[3:4, :] * ext[8:, :] + prm_ref[4:5, :]
    for back in (1, 2, 3):
        here = (pos >= back).astype(F32)
        pre = pre + prm_ref[3 - back : 4 - back, :] * (ext[8 - back : 8 - back + rows, :] * here)
    sig = jax.nn.sigmoid(pre)
    act = pre * sig
    xc = act[:, :width]
    state_size = (act.shape[1] - width) // 2
    b_rows = act[:, width : width + state_size].astype(BF16)
    c_rows = act[:, width + state_size :].astype(BF16)
    raw = dt_ref[...].astype(F32) + head_ref[0:1, :]
    dt = jnp.maximum(raw, 0.0) + jnp.log1p(jnp.exp(-jnp.abs(raw)))
    log_decay = -dt * head_ref[1:2, :]
    t_idx = lax.broadcasted_iota(jnp.int32, (rows, rows), 0)
    s_idx = lax.broadcasted_iota(jnp.int32, (rows, rows), 1)
    lower = (s_idx <= t_idx).astype(F32)
    cum = lax.dot_general(
        lower, log_decay, (((1,), (0,)), ((), ())), precision=HIGHEST, preferred_element_type=F32
    )
    same = (s_idx <= t_idx) & (s_idx >= t_idx - pos)
    scores = jnp.where(same, dot(c_rows, b_rows, CONTRACT_LAST), 0.0)
    t_col = lax.broadcasted_iota(jnp.int32, (rows, 1), 0)
    pos_last = pos[rows - 1 : rows, :]
    cum_last = cum[rows - 1 : rows, :]
    inward = jnp.exp(cum) * (pos > t_col).astype(F32)
    tail = jnp.exp(cum_last - cum) * (t_col >= rows - 1 - pos_last).astype(F32)
    carried = jnp.exp(cum_last) * (pos_last >= rows).astype(F32)
    wide = dot(
        two_parts(jnp.concatenate([dt, inward, tail, jnp.broadcast_to(carried, (8, LANES))], axis=0)),
        expand_ref[...],
    )
    return dict(
        pos=pos,
        pre=pre,
        sig=sig,
        xc=xc,
        b=b_rows,
        c=c_rows,
        raw=raw,
        dt=dt,
        log_decay=log_decay,
        cum=cum,
        cum_t=cum.T,
        same=same,
        scores=scores,
        carried=carried,
        t_idx=t_idx,
        s_idx=s_idx,
        dt_w=wide[:rows],
        in_w=wide[rows : 2 * rows],
        tail_w=wide[2 * rows : 3 * rows],
        carried_w=wide[3 * rows : 3 * rows + 1],
    )


def decay_of(k, head):
    return jnp.exp(jnp.minimum(k["cum"][:, head : head + 1] - k["cum_t"][head : head + 1, :], 0.0))


def halves(pair):
    lane = lax.broadcasted_iota(jnp.int32, pair.shape, 1)
    zero = jnp.zeros_like(pair)
    return jnp.concatenate(
        [jnp.where(lane < LANES // 2, pair, zero), jnp.where(lane < LANES // 2, zero, pair)], axis=0
    )


def forward_kernel(
    width, order, z_ref, x_ref, bc_ref, dt_ref, halo_x_ref, halo_bc_ref, pos_ref, prm_ref, head_ref,
    expand_ref, y_ref, g_ref, sum_ref, state_ref, ext, state,
):
    @pl.when(pl.program_id(0) == 0)
    def _():
        state[...] = jnp.zeros_like(state)

    k = prepare_chunk(
        width, x_ref, bc_ref, dt_ref, halo_x_ref, halo_bc_ref, pos_ref, prm_ref, head_ref, expand_ref, ext
    )
    rows = x_ref.shape[0]
    stepped = (k["xc"] * k["dt_w"]).astype(BF16)
    held = state[...]
    held_low = held.astype(BF16)
    state_ref[0] = held_low
    reached = dot(k["c"], held_low) * k["in_w"]
    weighted = (stepped.astype(F32) * k["tail_w"]).astype(BF16)
    state[...] = k["carried_w"] * held + dot(k["b"], weighted, CONTRACT_FIRST)
    for pair in range(width // LANES):
        lanes = slice(pair * LANES, (pair + 1) * LANES)
        mixing = jnp.concatenate(
            [
                (decay_of(k, 2 * pair) * k["scores"]).astype(BF16),
                (decay_of(k, 2 * pair + 1) * k["scores"]).astype(BF16),
            ],
            axis=1,
        )
        y_ref[:, lanes] = dot(mixing, halves(stepped[:, lanes])) + reached[:, lanes]
    z = z_ref[...].astype(F32)
    g = (y_ref[...] + prm_ref[6:7, :width] * k["xc"]) * (z * jax.nn.sigmoid(z))
    g_ref[...] = g
    total = jnp.sum(g * g, axis=1, keepdims=True)
    sum_ref[...] = jnp.broadcast_to(total, (rows, LANES)).T[:8, :]


def backward_kernel(
    width, chunks, order, z_ref, x_ref, bc_ref, dt_ref, halo_x_ref, halo_bc_ref, pos_ref, prm_ref, head_ref,
    expand_ref, y_ref, g_ref, state_ref, dyo_ref, coef_ref, grad_ref, small_ref, ext, d_state, later, later_pos,
):
    first = pl.program_id(0) == 0

    @pl.when(first)
    def _():
        d_state[...] = jnp.zeros_like(d_state)
        later[...] = jnp.zeros_like(later)
        later_pos[...] = jnp.zeros_like(later_pos)
        small_ref[...] = jnp.zeros_like(small_ref)

    k = prepare_chunk(
        width, x_ref, bc_ref, dt_ref, halo_x_ref, halo_bc_ref, pos_ref, prm_ref, head_ref, expand_ref, ext
    )
    rows = x_ref.shape[0]
    xc = k["xc"]
    z = z_ref[...].astype(F32)
    sig_z = jax.nn.sigmoid(z)
    r_col = coef_ref[:, 0:1]
    back_col = coef_ref[:, 1:2]
    g = g_ref[...]
    y = y_ref[...]
    dyo = dyo_ref[...].astype(F32)
    skip = prm_ref[6:7, :width]
    dg = r_col * (dyo * prm_ref[5:6, :width]) - g * back_col
    dy = dg * (z * sig_z)
    grad_ref[:, :width] = (dg * (y + skip * xc) * (sig_z * (1.0 + z * (1.0 - sig_z)))).astype(BF16)
    small_ref[5:6, :width] += jnp.sum(dyo * g * r_col, axis=0, keepdims=True)
    small_ref[6:7, :width] += jnp.sum(dy * xc, axis=0, keepdims=True)

    stepped = (xc * k["dt_w"]).astype(BF16)
    dy_low = dy.astype(BF16)
    d_held = d_state[...]
    d_held_low = d_held.astype(BF16)
    held_low = state_ref[0]
    weighted = (stepped.astype(F32) * k["tail_w"]).astype(BF16)
    dy_in = (dy * k["in_w"]).astype(BF16)
    from_state = dot(k["b"], d_held_low) * k["tail_w"]
    dc = dot(dy_in, held_low, CONTRACT_LAST)
    db = dot(weighted, d_held_low, CONTRACT_LAST)
    d_state[...] = k["carried_w"] * d_held + dot(k["c"], dy_in, CONTRACT_FIRST)
    d_scores = jnp.zeros((rows, rows), F32)
    d_stepped = []
    for pair in range(width // LANES):
        lanes = slice(pair * LANES, (pair + 1) * LANES)
        decay_a = decay_of(k, 2 * pair)
        decay_b = decay_of(k, 2 * pair + 1)
        mixing = jnp.concatenate(
            [(decay_a * k["scores"]).astype(BF16), (decay_b * k["scores"]).astype(BF16)], axis=0
        )
        d_mixing = dot(dy_low[:, lanes], halves(stepped[:, lanes]), CONTRACT_LAST)
        d_scores = d_scores + decay_a * d_mixing[:, :rows] + decay_b * d_mixing[:, rows:]
        d_stepped.append(dot(mixing, halves(dy_low[:, lanes]), CONTRACT_FIRST))
    d_stepped = jnp.concatenate(d_stepped, axis=1) + from_state
    d_scores = jnp.where(k["same"], d_scores, 0.0).astype(BF16)
    dc = dc + dot(d_scores, k["b"])
    db = db + dot(d_scores, k["c"], CONTRACT_FIRST)
    dxc = skip * dy + d_stepped * k["dt_w"]

    stepped_f = stepped.astype(F32)
    tail_term = jnp.sum(stepped_f * from_state, axis=0, keepdims=True) + k["carried_w"] * jnp.sum(
        held_low.astype(F32) * d_held, axis=0, keepdims=True
    )
    gathered = two_parts(
        jnp.concatenate(
            [
                d_stepped * xc,
                dy_low.astype(F32) * y - stepped_f * d_stepped,
                jnp.broadcast_to(tail_term, (8, width)),
            ],
            axis=0,
        )
    )
    expand = expand_ref[:LANES, :]
    narrow = dot(gathered[:, :width], expand, CONTRACT_LAST) + dot(gathered[:, width:], expand, CONTRACT_LAST)
    d_dt = narrow[:rows]
    d_cum = narrow[rows : 2 * rows]
    upper = (k["s_idx"] >= k["t_idx"]).astype(F32)
    d_decay = (
        lax.dot_general(
            upper, d_cum, (((1,), (0,)), ((), ())), precision=HIGHEST, preferred_element_type=F32
        )
        + narrow[2 * rows : 2 * rows + 1]
    )
    d_raw = (d_dt - d_decay * head_ref[1:2, :]) * jax.nn.sigmoid(k["raw"])
    small_ref[7:8, :LANES] += jnp.sum(d_raw, axis=0, keepdims=True)
    small_ref[7:8, LANES : 2 * LANES] += jnp.sum(d_decay * k["log_decay"], axis=0, keepdims=True)
    conv_end = grad_ref.shape[1] - LANES
    grad_ref[:, conv_end:] = d_raw.astype(BF16)

    pre, sig, pos = k["pre"], k["sig"], k["pos"]
    d_pre = jnp.concatenate([dxc, db, dc], axis=1) * (sig * (1.0 + pre * (1.0 - sig)))
    small_ref[4:5, :] += jnp.sum(d_pre, axis=0, keepdims=True)
    later[:rows, :] = d_pre
    later_pos[:rows, :] = jnp.broadcast_to(pos, (rows, LANES))
    d_in = prm_ref[3:4, :] * d_pre
    small_ref[3:4, :] += jnp.sum(d_pre * ext[8:, :], axis=0, keepdims=True)
    for back in (1, 2, 3):
        here = (pos >= back).astype(F32)
        small_ref[3 - back : 4 - back, :] += jnp.sum(
            d_pre * (ext[8 - back : 8 - back + rows, :] * here), axis=0, keepdims=True
        )
        there = (later_pos[back : back + rows, 0:1] >= back).astype(F32)
        d_in = d_in + prm_ref[3 - back : 4 - back, :] * (later[back : back + rows, :] * there)
    grad_ref[:, width:conv_end] = d_in.astype(BF16)
    later[rows:, :] = later[:8, :]
    later_pos[rows:, :] = later_pos[:8, :]


def token_specs(width, chunks, per_block, reverse):
    def at(step):
        return chunks - 1 - step if reverse else step

    def place(step, order):
        chunk = at(step)
        return order[chunk // per_block] * per_block + chunk % per_block

    def before(step, order):
        tile = jnp.maximum(at(step) * (CHUNK // 16) - 1, 0)
        tiles = per_block * (CHUNK // 16)
        return order[tile // tiles] * tiles + tile % tiles

    bc = 2 * LANES
    specs = [
        pl.BlockSpec((CHUNK, width), lambda i, o: (place(i, o), 0)),
        pl.BlockSpec((CHUNK, width), lambda i, o: (place(i, o), 1)),
        pl.BlockSpec((CHUNK, bc), lambda i, o: (place(i, o), 2 * width // bc)),
        pl.BlockSpec((CHUNK, LANES), lambda i, o: (place(i, o), (2 * width + bc) // LANES)),
        pl.BlockSpec((16, width), lambda i, o: (before(i, o), 1)),
        pl.BlockSpec((16, bc), lambda i, o: (before(i, o), 2 * width // bc)),
        pl.BlockSpec((CHUNK, 1), lambda i, o: (at(i), 0)),
        pl.BlockSpec((8, width + bc), lambda i, o: (0, 0)),
        pl.BlockSpec((8, LANES), lambda i, o: (0, 0)),
        pl.BlockSpec((2 * LANES, width), lambda i, o: (0, 0)),
    ]
    return specs, place, at


def mixer_forward(width, order, projected, pos, prm, head_prm, expand):
    rows = projected.shape[0]
    chunks = rows // CHUNK
    per_block = chunks // order.shape[0]
    specs, place, at = token_specs(width, chunks, per_block, False)
    return pl.pallas_call(
        functools.partial(forward_kernel, width),
        out_shape=(
            jax.ShapeDtypeStruct((rows, width), F32),
            jax.ShapeDtypeStruct((rows, width), F32),
            jax.ShapeDtypeStruct((8, rows), F32),
            jax.ShapeDtypeStruct((chunks, LANES, width), BF16),
        ),
        grid_spec=pltpu.PrefetchScalarGridSpec(
            num_scalar_prefetch=1,
            grid=(chunks,),
            in_specs=specs,
            out_specs=(
                pl.BlockSpec((CHUNK, width), lambda i, o: (place(i, o), 0)),
                pl.BlockSpec((CHUNK, width), lambda i, o: (place(i, o), 0)),
                pl.BlockSpec((8, CHUNK), lambda i, o: (0, place(i, o))),
                pl.BlockSpec((1, LANES, width), lambda i, o: (i, 0, 0)),
            ),
            scratch_shapes=[
                pltpu.VMEM((CHUNK + 8, width + 2 * LANES), F32),
                pltpu.VMEM((LANES, width), F32),
            ],
        ),
        compiler_params=pltpu.CompilerParams(
            dimension_semantics=("arbitrary",), vmem_limit_bytes=40 * 1024 * 1024
        ),
        cost_estimate=pl.CostEstimate(flops=rows * width * 1024, bytes_accessed=rows * width * 14, transcendentals=0),
    )(order, projected, projected, projected, projected, projected, projected, pos, prm, head_prm, expand)


def mixer_backward(width, order, projected, pos, prm, head_prm, expand, y, g, states, dyo, coef):
    rows, columns = projected.shape
    chunks = rows // CHUNK
    per_block = chunks // order.shape[0]
    specs, place, at = token_specs(width, chunks, per_block, True)
    wide = pl.BlockSpec((CHUNK, width), lambda i, o: (place(i, o), 0))
    return pl.pallas_call(
        functools.partial(backward_kernel, width, chunks),
        out_shape=(
            jax.ShapeDtypeStruct((rows, columns), BF16),
            jax.ShapeDtypeStruct((8, width + 2 * LANES), F32),
        ),
        grid_spec=pltpu.PrefetchScalarGridSpec(
            num_scalar_prefetch=1,
            grid=(chunks,),
            in_specs=specs
            + [
                wide,
                wide,
                pl.BlockSpec((1, LANES, width), lambda i, o: (at(i), 0, 0)),
                wide,
                pl.BlockSpec((CHUNK, 8), lambda i, o: (place(i, o), 0)),
            ],
            out_specs=(
                pl.BlockSpec((CHUNK, columns), lambda i, o: (place(i, o), 0)),
                pl.BlockSpec((8, width + 2 * LANES), lambda i, o: (0, 0)),
            ),
            scratch_shapes=[
                pltpu.VMEM((CHUNK + 8, width + 2 * LANES), F32),
                pltpu.VMEM((LANES, width), F32),
                pltpu.VMEM((CHUNK + 8, width + 2 * LANES), F32),
                pltpu.VMEM((CHUNK + 8, LANES), jnp.int32),
            ],
        ),
        compiler_params=pltpu.CompilerParams(
            dimension_semantics=("arbitrary",), vmem_limit_bytes=48 * 1024 * 1024
        ),
        cost_estimate=pl.CostEstimate(flops=rows * width * 2048, bytes_accessed=rows * width * 20, transcendentals=0),
    )(order, projected, projected, projected, projected, projected, projected, pos, prm, head_prm, expand,
      y, g, states, dyo, coef)


def swap(array, axis, bits):
    return lax.ppermute(array, axis, [(i, i ^ bits) for i in range(lax.axis_size(axis))])


def gather_tp(block):
    if lax.axis_size("tp") != 4:
        return lax.all_gather(block, "tp", axis=0, tiled=True)
    half = block.shape[0] // 2
    a = swap(block, "tp", 1)
    b = swap(block, "tp", 2)
    c = swap(a[:half], "tp", 2)
    d = swap(b[half:], "tp", 1)
    return jnp.concatenate([block, a, b, c, d], axis=0)


def scatter_tp(blocks):
    if lax.axis_size("tp") != 4:
        return lax.psum_scatter(jnp.concatenate(blocks, axis=0), "tp", scatter_dimension=0, tiled=True).astype(F32)
    half = blocks[0].shape[0] // 2
    a = swap(blocks[3][:half], "tp", 1)
    b = swap(blocks[3][half:], "tp", 2)
    to_1 = jnp.concatenate([blocks[1][:half], blocks[1][half:] + b], axis=0)
    to_2 = jnp.concatenate([blocks[2][:half] + a, blocks[2][half:]], axis=0)
    c = swap(to_1, "tp", 1)
    d = swap(to_2, "tp", 2)
    return blocks[0].astype(F32) + c.astype(F32) + d.astype(F32)


def sum_tp(array):
    if lax.axis_size("tp") != 4:
        return lax.psum(array, "tp")
    parts = jnp.split(array, 4, axis=-1)
    total = array
    for bits in (1, 2, 3):
        total = total + swap(jnp.concatenate([parts[k ^ bits] for k in range(4)], axis=-1), "tp", bits)
    return total


def in_norm_scale(values):
    return lax.rsqrt(jnp.mean(values * values, axis=-1, keepdims=True) + EPSILON)


def body(
    x_in, norm_gain, w_z, w_x, w_b, w_c, w_dt, conv_w, conv_b, dt_bias, a_log, d_skip, gate_gain, w_out,
    doc_lens, d_out,
):
    tp_count = lax.axis_size("tp")
    rank = lax.axis_index("tp")
    dev_rows, model = x_in.shape
    rows = dev_rows * tp_count
    inner = gate_gain.shape[0]
    width = w_z.shape[1]
    heads = w_dt.shape[1]
    state_size = (conv_w.shape[0] - inner) // 2
    head_size = width // heads
    own_cols = w_b.shape[1]
    order = jnp.arange(tp_count, dtype=jnp.int32)
    if tp_count == 4:
        order = order ^ rank.astype(jnp.int32)

    x_float = x_in.astype(F32)
    r_in = in_norm_scale(x_float)
    normed = (x_float * r_in * norm_gain[None, :]).astype(BF16)

    w_bc_own = jnp.concatenate([w_b, w_c], axis=1).T
    w_bc_all = lax.all_gather(w_bc_own, "tp", axis=0) if tp_count != 4 else None
    if tp_count == 4:
        parts = jnp.stack([w_bc_own] + [swap(w_bc_own, "tp", bits) for bits in (1, 2, 3)])
        w_bc_all = jnp.stack([lax.dynamic_index_in_dim(parts, order[j], 0, False) for j in range(4)])
    w_bc_all = w_bc_all.reshape(tp_count, 2, own_cols, model)
    w_bc = jnp.swapaxes(w_bc_all, 0, 1).reshape(2 * state_size, model).T
    w_joined = jnp.concatenate(
        [w_z, w_x, w_bc, w_dt, jnp.zeros((model, LANES - heads), BF16)], axis=1
    )
    gathered = gather_tp(normed)
    projected = dot(gathered, w_joined).astype(BF16)

    lengths = doc_lens[0]
    doc_starts = jnp.cumsum(lengths) - lengths
    positions = jnp.arange(rows, dtype=jnp.int32)
    started = jnp.where(positions[:, None] >= doc_starts[None, :], doc_starts[None, :], 0)
    pos = (positions - jnp.max(started, axis=1))[:, None]

    def own(array, count):
        return lax.dynamic_slice_in_dim(array, rank * count, count, axis=0)

    taps = jnp.concatenate([own(conv_w[:inner], width), conv_w[inner:]], axis=0).T
    bias = jnp.concatenate([own(conv_b[:inner], width), conv_b[inner:]])
    pad_bc = jnp.zeros((2 * state_size,), F32)
    gain_own = own(gate_gain, width)
    skip_own = jnp.repeat(own(d_skip, heads), head_size)
    prm = jnp.concatenate(
        [
            taps,
            bias[None],
            jnp.concatenate([gain_own, pad_bc])[None],
            jnp.concatenate([skip_own, pad_bc])[None],
            jnp.zeros((1, width + 2 * state_size), F32),
        ],
        axis=0,
    )
    pad_heads = jnp.zeros((LANES - heads,), F32)
    head_prm = jnp.concatenate(
        [
            jnp.concatenate([own(dt_bias, heads), pad_heads])[None],
            jnp.concatenate([jnp.exp(own(a_log, heads)), pad_heads])[None],
            jnp.zeros((6, LANES), F32),
        ],
        axis=0,
    )
    expand = (
        (jnp.arange(2 * LANES) % LANES)[:, None] == (jnp.arange(width) // head_size)[None, :]
    ).astype(BF16)

    y, g, g_sum, states = mixer_forward(width, order, projected, pos, prm, head_prm, expand)
    d_held, _ = lax.optimization_barrier((d_out, gathered))
    grad_gathered = gather_tp(d_held)
    g_total = sum_tp(g_sum)[0]
    r_gate = lax.rsqrt(g_total / inner + EPSILON)
    dyo = dot(grad_gathered, w_out, CONTRACT_LAST).astype(BF16)
    eg_sum = jnp.sum(dyo.astype(F32) * gain_own[None, :] * g, axis=1)
    eg_total = sum_tp(eg_sum)
    coef = jnp.stack([r_gate, r_gate**3 * (eg_total / inner)] + [jnp.zeros_like(r_gate)] * 6, axis=1)
    yo = (g * r_gate[:, None] * gain_own[None, :]).astype(BF16)
    yo = lax.optimization_barrier(yo)

    def block(array, k):
        return array[k * dev_rows : (k + 1) * dev_rows]

    out_parts = [dot(block(yo, k), w_out).astype(BF16) for k in range(tp_count)]
    block_out = (x_float + scatter_tp(out_parts)).astype(BF16)

    grad_projected, small = mixer_backward(
        width, order, projected, pos, prm, head_prm, expand, y, g, states, dyo, coef
    )

    def scatter_dp(partial):
        return lax.psum_scatter(partial.astype(BF16), "dp", scatter_dimension=0, tiled=True).astype(F32)

    grad_w_out = scatter_dp(dot(grad_gathered, yo, CONTRACT_FIRST)).T
    grad_w_z = scatter_dp(dot(gathered, grad_projected[:, :width], CONTRACT_FIRST))

    d_bc = grad_projected[:, 2 * width : 2 * width + 2 * state_size]
    d_dt = grad_projected[:, 2 * width + 2 * state_size : 2 * width + 2 * state_size + heads]
    by_owner = jnp.moveaxis(d_bc.reshape(rows, 2, tp_count, own_cols), 2, 0).reshape(tp_count, rows, 2 * own_cols)
    if tp_count == 4:
        d_bc_own = lax.dynamic_index_in_dim(by_owner, rank, 0, False).astype(F32)
        for bits in (1, 2, 3):
            sent = lax.dynamic_index_in_dim(by_owner, order[bits], 0, False)
            sent = sent.reshape(tp_count, dev_rows, -1)
            sent = jnp.stack([sent[k ^ bits] for k in range(tp_count)]).reshape(rows, -1)
            d_bc_own = d_bc_own + swap(sent, "tp", bits).astype(F32)
    else:
        d_bc_own = lax.psum_scatter(by_owner.astype(F32), "tp", scatter_dimension=0, tiled=False)
    last = jnp.concatenate(
        [
            grad_projected[:, width : 2 * width],
            d_bc_own.astype(BF16),
            d_dt,
            jnp.zeros((rows, (-2 * own_cols - heads) % LANES), BF16),
        ],
        axis=1,
    )
    grad_last = scatter_dp(dot(gathered, last, CONTRACT_FIRST))

    du_parts = [dot(block(grad_projected, k), w_joined, CONTRACT_LAST) for k in range(tp_count)]
    gain_part = sum(
        jnp.sum(du_parts[k] * block(gathered, k).astype(F32), axis=0) for k in range(tp_count)
    ) / norm_gain
    du = scatter_tp([part.astype(BF16) for part in du_parts])
    e_in = du * norm_gain[None, :]
    grad_x = d_out.astype(F32) + r_in * e_in - x_float * (
        r_in**3 * jnp.mean(e_in * x_float, axis=-1, keepdims=True)
    )

    per_head = small[6, :width].reshape(heads, head_size).sum(axis=1)
    own_small = jnp.concatenate(
        [small[:6, :width].reshape(-1), small[7, :heads], small[7, LANES : LANES + heads], per_head]
    )
    shared_small = jnp.concatenate([small[:5, width:].reshape(-1), gain_part])
    own_small = lax.psum(own_small, "dp")
    shared_small = lax.psum(shared_small, ("dp", "tp"))
    all_small = lax.all_gather(own_small, "tp")
    channels = all_small[:, : 6 * width].reshape(tp_count, 6, width)
    channels = jnp.swapaxes(channels, 0, 1).reshape(6, inner)
    rest = all_small[:, 6 * width :].reshape(tp_count, 3, heads)
    rest = jnp.swapaxes(rest, 0, 1).reshape(3, heads * tp_count)
    shared = shared_small[: 5 * 2 * state_size].reshape(5, 2 * state_size)
    grad_conv = jnp.concatenate([channels[:5], shared], axis=1)
    return (
        block_out,
        grad_x,
        shared_small[5 * 2 * state_size :],
        grad_w_z,
        grad_last[:, :width],
        grad_last[:, width : width + own_cols],
        grad_last[:, width + own_cols : width + 2 * own_cols],
        grad_last[:, width + 2 * own_cols : width + 2 * own_cols + heads],
        grad_conv[:4].T,
        grad_conv[4],
        rest[0],
        rest[1],
        rest[2],
        channels[5],
        grad_w_out,
    )


def solution(mesh):
    rows = P(("dp", "tp"), None)
    columns = P(None, "tp")
    both = P("dp", "tp")
    none = P()
    return jax.shard_map(
        body,
        mesh=mesh,
        in_specs=(
            rows, none, columns, columns, columns, columns, columns, none, none, none, none, none, none,
            P("tp", None), P("dp", None), rows,
        ),
        out_specs=(
            rows, rows, none, both, both, both, both, both, none, none, none, none, none, none, P("tp", "dp"),
        ),
        check_vma=False,
    )
```

time: 1460 us -> 416 us (0.28)
  waiting for transfers between devices: 756 us -> 52.4 us
  local copies, waits for them, and re-layouts: 230 us -> 60.3 us
  other arithmetic: 130 us -> 23.3 us
  matrix products: 193 us -> 87.7 us
  Pallas kernels: 0 us -> 51.3 us
  blocking collectives: 99.9 us -> 78.1 us
  starting transfers between devices: 16.5 us -> 36.2 us
    reduce_scatter x3, waiting for transfers between devices: 298 us -> 0.01 us  [scatter_dp(): lax.psum_scatter(partial.astype(BF16), 'dp', scatter_dimension=0, tiled=T...]
    all_to_all x3 -> x0, waiting for transfers between devices: 247 us -> none  [the longest x1 141 us: body(): lax.all_to_all(outgoing, 'tp', split_axis=2, concat_axis=0, tiled=True)]
    psum x1 -> x0, waiting for transfers between devices: 115 us -> none  [body(): lax.psum((grad_norm_gain, grad_conv_w, grad_conv_b, grad_dt_bias, grad_a_...]
    dot_general x20 -> x13, matrix products: 193 us -> 87.7 us  [dot(): return lax.dot_general(a, b, dims, preferred_element_type=F32)]
    all_gather x4 -> x0, waiting for transfers between devices: 95.1 us -> none  [the longest x2 54.7 us: entering_2(): everything = jax.tree.map(lambda part: lax.all_gather(part, axis), array)]
    reshape x14 -> x5, local copies, waits for them, and re-layouts: 74.9 us -> 0.23 us  [the longest x1 0.08 us: body(): rest = all_small[:, 6 * width:].reshape(tp_count, 3, heads)]
    ppermute x0 -> x28, waiting for transfers between devices: none -> 52.4 us  [swap(): lax.ppermute(array, axis, [(i, i ^ bits) for i in range(lax.axis_size(axi...]
    pallas_call x0 -> x2, Pallas kernels: none -> 51.3 us  [the longest x1 36.7 us: mixer_backward(): pl.pallas_call(functools.partial(backward_kernel, width, chunks), out_sha...]
  transfers between devices with their start and end apart: 11 -> 31, of which waited for: 9 -> 11; matrix products, arithmetic and copies ran while one was open for 15% -> 34% of each run, Pallas kernels for 0% -> 12%
where the time goes in v1:
time: 416 us; the launch traced here: 412 us
  matrix products  87.7 us (21%)
  blocking collectives  78.1 us (19%)
  local copies, waits for them, and re-layouts  60.3 us (14%)
  waiting for transfers between devices  52.4 us (13%)
  Pallas kernels  51.3 us (12%)
  starting transfers between devices  36.2 us (9%)
  other arithmetic  23.3 us (6%)
  between operations  22.6 us (5%)
    dot_general x13, matrix products, dot(): return lax.dot_general(a, b, dims, preferred_element_type=F32)  87.7 us
    ppermute x28, waiting for transfers between devices, swap(): lax.ppermute(array, axis, [(i, i ^ bits) for i in range(lax.axis_size(axi...  52.4 us
    psum x1, blocking collectives, body(): shared_small = lax.psum(shared_small, ('dp', 'tp'))  43.2 us
    pallas_call x1, Pallas kernels, mixer_backward(): pl.pallas_call(functools.partial(backward_kernel, width, chunks), out_sha...  36.7 us
    ppermute x28, starting transfers between devices, swap(): lax.ppermute(array, axis, [(i, i ^ bits) for i in range(lax.axis_size(axi...  35.8 us
    psum x1, blocking collectives, body(): own_small = lax.psum(own_small, 'dp')  26.8 us
    unnamed x73, local copies, waits for them, and re-layouts  17 us
    concatenate x1, local copies, waits for them, and re-layouts, body(): jnp.concatenate([w_z, w_x, w_bc, w_dt, jnp.zeros((model, LANES - heads),...  15 us
  transfers between devices with their start and end apart: 31, of which 11 were waited for; matrix products, arithmetic and copies ran while one was open for 34% of the time, Pallas kernels for 12%

profile of v1, /device:TPU:0, one launch (start us, length us, event | category | flops | bytes accessed | tf_op | source)
XLA Modules:
  0.0 412.0 jit_solution(6254126358450599365)
XLA Ops:
  9.2 3.0 collective-permute-start.4
  12.2 1.5 collective-permute-start.5
  13.7 1.5 fusion.1
  15.3 2.9 constant_dynamic-update-slice_fusion.4
  18.2 1.9 collective-permute-start
  20.1 1.5 collective-permute-start.1
  34.4 12.3 %collective-permute-done = bf16[256,2048]{1,0:T(8,128)(2,1)S(1)} collective-permute-done((bf16[256,2048]{1,0:T(8,128)(2,1)}, bf16[256,2048]{1,0:T(8,128)(2,1)S(1)}, u32[]{:S(2)}, u32[]{:S(2)}) %collective-permute-start) | collective-permute-done | bytes 1048608 | tf_op jit(solution)/shard_map/ppermute | solution.py:357
  47.5 1.8 collective-permute-start.2
  51.5 15.0 %concatenate.85 = bf16[2048,2432]{1,0:T(8,128)(2,1)} concatenate(bf16[2048,1024]{1,0:T(8,128)(2,1)} %param.18, bf16[2048,1024]{1,0:T(8,128)(2,1)} %param.19, bf16[2048,256]{1,0:T(8,128)(2,1)S(1)} %copy.90, bf16[2048,16]{1,0:T(8,128)(2,1)} %copy.91, bf16[2048,112]{1,0:T(8,128)(2,1)} %broadcast_in_dim.30), dimensions={1} | concatenate | bytes 19922944 | tf_op jit(solution)/shard_map/concatenate | solution.py:427
  66.5 1.2 slice.317
  67.7 1.6 collective-permute-start.3
  70.3 2.3 constant_dynamic-update-slice_fusion.2
  72.6 1.9 constant_dynamic-update-slice_fusion.1
  74.5 5.9 %collective-permute-done.3 = bf16[128,2048]{1,0:T(8,128)(2,1)S(1)} collective-permute-done((bf16[128,2048]{1,0:T(8,128)(2,1)S(1)}, bf16[128,2048]{1,0:T(8,128)(2,1)S(1)}, u32[]{:S(2)}, u32[]{:S(2)}) %collective-permute-start.3) | collective-permute-done | bytes 524320 | tf_op jit(solution)/shard_map/ppermute | solution.py:357
  81.3 1.5 collective-permute-start.14
  83.3 16.4 %convolution_convert_fusion.1.z_ref.x_ref.bc_ref.dt_ref.halo_x_ref.halo_bc_ref = bf16[1024,2432]{1,0:T(8,128)(2,1)} fusion(bf16[1024,2048]{1,0:T(8,128)(2,1)} %constant_dynamic-update-slice_fusion, bf16[2048,2432]{1,0:T(8,128)(2,1)} %concatenate.85), kind=kOutput, calls=%fused_computation.1 | convolution fusion | flops 10203037696 | bytes 19136512 | tf_op jit(solution)/shard_map/dot_general | solution.py:21
  99.7 14.6 %shard_map.271 = (f32[1024,1024]{1,0:T(8,128)S(1)}, f32[1024,1024]{1,0:T(8,128)S(1)}, f32[8,1024]{1,0:T(8,128)S(1)}, bf16[8,128,1024]{2,1,0:T(8,128)(2,1)S(1)}) custom-call(s32[4]{0:T(128)S(1)} %iota_xor_fusion.order, bf16[1024,2432]{1,0:T(8,128)(2,1)} %convolution_convert_fusion.1.z_ref.x_ref.bc_ref.dt_ref.halo_x_ref.halo_bc_ref, ...), custom_call_target="tpu_custom_call" | custom-call | flops 1073741824 | bytes 14680064 | tf_op jit(solution)/shard_map/pallas_call | solution.py:284
  114.3 1.3 copy-done.2
  115.6 1.6 collective-permute-start.8
  117.8 1.4 collective-permute-start.9
  119.4 1.6 collective-permute-start.16
  121.4 1.6 collective-permute-done.9
  123.1 1.6 collective-permute-start.17
  124.9 5.6 %collective-permute-done.16 = bf16[128,2048]{1,0:T(8,128)(2,1)S(1)} collective-permute-done((bf16[128,2048]{1,0:T(8,128)(2,1)S(1)}, bf16[128,2048]{1,0:T(8,128)(2,1)S(1)}, u32[]{:S(2)}, u32[]{:S(2)}) %collective-permute-start.16) | collective-permute-done | bytes 524320 | tf_op jit(solution)/shard_map/ppermute | solution.py:357
  130.6 2.2 collective-permute-done.17
  132.9 8.4 %multiply_reduce_fusion = (f32[1024]{0:T(1024)S(1)}, bf16[1024,1024]{1,0:T(8,128)(2,1)S(1)}, bf16[1024,1024]{1,0:T(8,128)(2,1)}) fusion(f32[1024,1024]{1,0:T(8,128)S(1)} %get-tuple-element.22.g_ref, f32[1024]{0:T(1024)S(1)} %dynamic_slice.50, f32[1024]{0:T(1024)S(1)} %bitcast.91, bf16[1024,2048]{1,0:T(8,128)(2,1)S(1)} %constant_dynamic-update-slice_fusion.7, ...), kind=kOutput, calls=%fused_computation.2 | convolution fusion | flops 4303354880 | bytes 16789504 | tf_op jit(solution)/shard_map/dot_general | solution.py:21
  141.3 6.3 %convolution_convert_fusion.2 = bf16[2048,1024]{1,0:T(8,128)(2,1)} fusion(bf16[1024,2048]{1,0:T(8,128)(2,1)S(1)} %constant_dynamic-update-slice_fusion.7, bf16[1024,1024]{1,0:T(8,128)(2,1)S(1)} %get-tuple-element.112), kind=kOutput, calls=%fused_computation.9 | convolution fusion | flops 4297064448 | bytes 10485760 | tf_op jit(solution)/shard_map/dot_general | solution.py:21
  148.5 1.1 collective-permute-start.18
  149.6 1.7 collective-permute-start.20
  152.1 2.0 collective-permute-done.20
  154.4 1.6 copy-done.3
  156.0 1.6 copy-done.4
  157.6 36.7 %shard_map.272 = (bf16[1024,2432]{1,0:T(8,128)(2,1)}, f32[8,1280]{1,0:T(8,128)S(1)}) custom-call(s32[4]{0:T(128)S(1)} %iota_xor_fusion.order, bf16[1024,2432]{1,0:T(8,128)(2,1)} %convolution_convert_fusion.1.z_ref.x_ref.bc_ref.dt_ref.halo_x_ref.halo_bc_ref, bf16[1024,2432]{1,0:T(8,128)(2,1)} %convolution_convert_fusion.1.z_ref.x_ref.bc_ref.dt_ref.halo_x_ref.halo_bc_ref, ...), custom_call_target="tpu_custom_call" | custom-call | flops 2147483648 | bytes 20971520 | tf_op jit(solution)/shard_map/pallas_call | solution.py:320
  194.3 7.8 %convolution_convert_fusion.3 = bf16[2048,1024]{1,0:T(8,128)(2,1)} fusion(bf16[1024,2048]{1,0:T(8,128)(2,1)S(1)} %copy-done.16, bf16[1024,2432]{1,0:T(8,128)(2,1)} %get-tuple-element.27), kind=kOutput, calls=%fused_computation.10 | convolution fusion | flops 4297064448 | bytes 10485760 | tf_op jit(solution)/shard_map/dot_general | solution.py:21
  202.3 1.3 copy-done.25
  203.7 3.6 convolution_convert_fusion.5
  208.3 1.7 collective-permute-start.10
  210.7 2.3 convolution_convert_fusion.6
  213.0 2.3 convolution_convert_fusion.4
  215.3 2.6 fusion
  220.2 1.3 collective-permute-start.25
  223.5 1.9 collective-permute-start.27
  225.4 1.8 slice.281
  228.7 3.1 collective-permute-done.26
  231.8 1.2 fusion.22
  233.0 3.6 concatenate.107
  236.6 9.6 %convolution_convert_fusion = bf16[2048,1152]{1,0:T(8,128)(2,1)} fusion(bf16[1024,2048]{1,0:T(8,128)(2,1)} %constant_dynamic-update-slice_fusion, bf16[1024,1152]{1,0:T(8,128)(2,1)} %concatenate.107), kind=kOutput, calls=%fused_computation | convolution fusion | flops 4834197504 | bytes 11272192 | tf_op jit(solution)/shard_map/dot_general | solution.py:21
  246.3 26.8 %psum.15 = f32[1,6192]{1,0:T(1,128)S(1)} all-reduce(f32[1,6192]{1,0:T(1,128)S(1)} %all_gather.6), channel_id=1, replica_groups=mesh['dp'=8,'tp'=4] {'dp'}, use_global_device_ids=true, to_apply=%region_13.14 | all-reduce | flops 6192 | bytes 49536 | tf_op jit(solution)/shard_map/psum | solution.py:536
  273.1 8.0 %all-gather = f32[4,1,6192]{2,1,0:T(1,128)S(1)} all-gather(f32[1,1,6192]{2,1,0:T(1,128)S(1)} %bitcast.90), channel_id=1, replica_groups=mesh['dp'=8,'tp'=4] {'tp'}, dimensions={0}, use_global_device_ids=true | all-gather | bytes 123840 | tf_op jit(solution)/shard_map/all_gather | solution.py:538
  281.3 7.4 %multiply_reduce_fusion.1 = (f32[2048]{0:T(1024)S(1)}, bf16[256,2048]{1,0:T(8,128)(2,1)S(1)}) fusion(bf16[128,2048]{1,0:T(8,128)(2,1)S(1)} %copy-done.15, bf16[128,2048]{1,0:T(8,128)(2,1)} %collective-permute-done.2, bf16[2048,2432]{1,0:T(8,128)(2,1)} %concatenate.85, bf16[1024,2432]{1,0:T(8,128)(2,1)} %get-tuple-element.27), kind=kOutput, calls=%fused_computation.23 | convolution fusion | flops 2553804800 | bytes 13312000 | tf_op jit(solution)/shard_map/dot_general | solution.py:21
  294.1 7.3 %multiply_reduce_fusion.3 = (f32[2048]{0:T(1024)S(1)}, bf16[256,2048]{1,0:T(8,128)(2,1)S(1)}) fusion(bf16[256,2048]{1,0:T(8,128)(2,1)S(1)} %copy-done.10, bf16[2048,2432]{1,0:T(8,128)(2,1)} %concatenate.85, bf16[1024,2432]{1,0:T(8,128)(2,1)} %get-tuple-element.27), kind=kOutput, calls=%fused_computation.25 | convolution fusion | flops 2552231936 | bytes 13312000 | tf_op jit(solution)/shard_map/dot_general | solution.py:21
  301.3 7.6 %multiply_reduce_fusion.2 = (f32[2048]{0:T(1024)S(1)}, bf16[256,2048]{1,0:T(8,128)(2,1)S(1)}) fusion(bf16[256,2048]{1,0:T(8,128)(2,1)} %collective-permute-done.1, bf16[2048,2432]{1,0:T(8,128)(2,1)} %concatenate.85, bf16[1024,2432]{1,0:T(8,128)(2,1)} %get-tuple-element.27), kind=kOutput, calls=%fused_computation.24 | convolution fusion | flops 2552231936 | bytes 13312000 | tf_op jit(solution)/shard_map/dot_general | solution.py:21
  309.1 1.2 collective-permute-start.22
  311.5 1.1 fusion.35
  314.8 1.1 slice_add_fusion.2
  317.9 17.3 %collective-permute-done.22 = bf16[256,2048]{1,0:T(8,128)(2,1)S(1)} collective-permute-done((bf16[256,2048]{1,0:T(8,128)(2,1)S(1)}, bf16[256,2048]{1,0:T(8,128)(2,1)S(1)}, u32[]{:S(2)}, u32[]{:S(2)}) %collective-permute-start.22) | collective-permute-done | bytes 1048608 | tf_op jit(solution)/shard_map/ppermute | solution.py:357
  335.3 1.4 collective-permute-done.24
  336.7 6.3 %multiply_reduce_fusion.4 = (f32[2048]{0:T(1024)S(1)}, f32[256]{0:T(256)S(1)}, bf16[256,2048]{1,0:T(8,128)(2,1)}) fusion(bf16[256,2048]{1,0:T(8,128)(2,1)} %get-tuple-element.110, bf16[256,2048]{1,0:T(8,128)(2,1)S(1)} %copy-done.5, f32[2048]{0:T(1024)S(1)} %copy-done.17, bf16[256,2048]{1,0:T(8,128)(2,1)S(1)} %collective-permute-done.24, ...), kind=kOutput, calls=%fused_computation.26 | convolution fusion | flops 2557474560 | bytes 16466944 | tf_op jit(solution)/shard_map/dot_general | solution.py:21
  343.1 43.2 %psum.14 = f32[3328]{0:T(1024)S(1)} all-reduce(f32[3328]{0:T(1024)S(1)} %pad_maximum_fusion.13), channel_id=1, replica_groups=mesh['dp'=8,'tp'=4] {'dp','tp'}, use_global_device_ids=true, to_apply=%region_9.10 | all-reduce | flops 3328 | bytes 26624 | tf_op jit(solution)/shard_map/psum | solution.py:537
  388.2 6.3 %fusion.6 = (f32[256,2048]{1,0:T(8,128)}, bf16[256,2048]{1,0:T(8,128)(2,1)}) fusion(bf16[256,2048]{1,0:T(8,128)(2,1)S(1)} %copy-done.5, bf16[256,2048]{1,0:T(8,128)(2,1)S(1)} %copy-done.7, bf16[256,2048]{1,0:T(8,128)(2,1)} %copy-done.11, bf16[256,2048]{1,0:T(8,128)(2,1)S(1)} %collective-permute-done.22, f32[256]{0:T(256)S(1)} %fusion.31, ...), kind=kLoop, calls=%fused_computation.21 | loop fusion | flops 9437184 | bytes 12593152 | tf_op jit(solution)/shard_map/sub | solution.py:527
  394.5 1.1 convert_bitcast_fusion
  395.6 1.3 copy.104
  397.0 2.1 convert_element_type.145
  403.1 2.1 slice.341
  (224 shorter events, 40.8 us)
Async XLA Ops:
  7.2 15.2 %slice-start.3 = ((f32[4352,4]{0,1:T(4,128)}), f32[4096,4]{0,1:T(4,128)S(1)}, s32[]{:S(2)}) async-start(f32[4352,4]{0,1:T(4,128)} %param.23), calls=%async_computation.9 | async-start | bytes 131072 | tf_op jit(solution)/shard_map/slice | solution.py:442
  7.2 15.6 %slice-start.4 = ((f32[4352,4]{0,1:T(4,128)}), f32[256,4]{0,1:T(4,128)S(1)}, s32[]{:S(2)}) async-start(f32[4352,4]{0,1:T(4,128)} %param.23), calls=%async_computation.10 | async-start | bytes 8192 | tf_op jit(solution)/shard_map/slice | solution.py:442
  7.2 15.2 %slice-start.5 = ((f32[4352]{0:T(1024)}), f32[4096]{0:T(1024)S(1)}, s32[]{:S(2)}) async-start(f32[4352]{0:T(1024)} %param.24), calls=%async_computation.11 | async-start | bytes 32768 | tf_op jit(solution)/shard_map/slice | solution.py:443
  7.2 15.8 %slice-start.6 = ((f32[4352]{0:T(1024)}), f32[256]{0:T(256)S(1)}, s32[]{:S(2)}) async-start(f32[4352]{0:T(1024)} %param.24), calls=%async_computation.12 | async-start | bytes 2048 | tf_op jit(solution)/shard_map/slice | solution.py:443
  7.2 15.0 %copy-start.20 = (f32[64]{0:T(128)S(1)}, f32[64]{0:T(128)}, u32[]{:S(2)}) copy-start(f32[64]{0:T(128)} %param.26) | copy-start | bytes 772
  7.2 15.1 %copy-start.21 = (f32[64]{0:T(128)S(1)}, f32[64]{0:T(128)}, u32[]{:S(2)}) copy-start(f32[64]{0:T(128)} %param.25) | copy-start | bytes 772
  7.2 15.2 %copy-start.22 = (s32[1,8]{1,0:T(1,128)S(1)}, s32[1,8]{1,0:T(1,128)}, u32[]{:S(2)}) copy-start(s32[1,8]{1,0:T(1,128)} %param.30) | copy-start | bytes 100
  7.3 21.0 %copy-start.18 = (bf16[2048,16]{0,1:T(8,128)(2,1)S(1)}, bf16[2048,16]{0,1:T(8,128)(2,1)}, u32[]{:S(2)}) copy-start(bf16[2048,16]{0,1:T(8,128)(2,1)} %param.22) | copy-start | bytes 196612
  7.3 22.7 %copy-start.23 = (f32[64]{0:T(128)S(1)}, f32[64]{0:T(128)}, u32[]{:S(2)}) copy-start(f32[64]{0:T(128)} %param.27) | copy-start | bytes 772
  7.3 387.2 %reduce-scatter.8.cloned.1.call-start = ((), (), s32[]{:S(2)}) async-start(), calls=%async_computation.5 | async-start | bytes 4718592 | tf_op jit(solution)/shard_map/reduce_scatter | solution.py:493
  9.2 24.0 %collective-permute-start.4 = (bf16[64,2048]{1,0:T(8,128)(2,1)S(1)}, bf16[64,2048]{1,0:T(8,128)(2,1)S(1)}, u32[]{:S(2)}, u32[]{:S(2)}) collective-permute-start(bf16[64,2048]{1,0:T(8,128)(2,1)S(1)} %bitcast.82), channel_id=1, source_target_pairs={{0,1},{1,0},{2,3},{3,2},{4,5},{5,4},{6,7},{7,6},{8,9},{9,8},{10,11... | collective-permute-start | bytes 786440 | tf_op jit(solution)/shard_map/ppermute | solution.py:357
  12.2 21.0 %collective-permute-start.5 = (bf16[64,2048]{1,0:T(8,128)(2,1)S(1)}, bf16[64,2048]{1,0:T(8,128)(2,1)S(1)}, u32[]{:S(2)}, u32[]{:S(2)}) collective-permute-start(bf16[64,2048]{1,0:T(8,128)(2,1)S(1)} %bitcast.83), channel_id=1, source_target_pairs={{0,2},{1,3},{2,0},{3,1},{4,6},{5,7},{6,4},{7,5},{8,10},{9,11},{10,... | collective-permute-start | bytes 786440 | tf_op jit(solution)/shard_map/ppermute | solution.py:357
  13.7 19.5 %collective-permute-start.6 = (bf16[64,2048]{1,0:T(8,128)(2,1)S(1)}, bf16[64,2048]{1,0:T(8,128)(2,1)}, u32[]{:S(2)}, u32[]{:S(2)}) collective-permute-start(bf16[64,2048]{1,0:T(8,128)(2,1)S(1)} %bitcast.84), channel_id=1, source_target_pairs={{0,3},{1,2},{2,1},{3,0},{4,7},{5,6},{6,5},{7,4},{8,11},{9,10},{10,... | collective-permute-start | bytes 786440 | tf_op jit(solution)/shard_map/ppermute | solution.py:357
  18.2 28.5 %collective-permute-start = (bf16[256,2048]{1,0:T(8,128)(2,1)}, bf16[256,2048]{1,0:T(8,128)(2,1)S(1)}, u32[]{:S(2)}, u32[]{:S(2)}) collective-permute-start(bf16[256,2048]{1,0:T(8,128)(2,1)} %get-tuple-element.110), channel_id=1, source_target_pairs={{0,1},{1,0},{2,3},{3,2},{4,5},{5,4},{6,7},{7,6},{8,9},{9,8},{10,11... | collective-permute-start | bytes 3145736 | tf_op jit(solution)/shard_map/ppermute | solution.py:357
  20.1 46.4 %collective-permute-start.1 = (bf16[256,2048]{1,0:T(8,128)(2,1)}, bf16[256,2048]{1,0:T(8,128)(2,1)}, u32[]{:S(2)}, u32[]{:S(2)}) collective-permute-start(bf16[256,2048]{1,0:T(8,128)(2,1)} %get-tuple-element.110), channel_id=1, source_target_pairs={{0,2},{1,3},{2,0},{3,1},{4,6},{5,7},{6,4},{7,5},{8,10},{9,11},{10,... | collective-permute-start | bytes 3145736 | tf_op jit(solution)/shard_map/ppermute | solution.py:357
  46.6 2.9 copy-start.8
  47.5 25.1 %collective-permute-start.2 = (bf16[128,2048]{1,0:T(8,128)(2,1)}, bf16[128,2048]{1,0:T(8,128)(2,1)}, u32[]{:S(2)}, u32[]{:S(2)}) collective-permute-start(bf16[128,2048]{1,0:T(8,128)(2,1)} %slice.316), channel_id=1, source_target_pairs={{0,2},{1,3},{2,0},{3,1},{4,6},{5,7},{6,4},{7,5},{8,10},{9,11},{10,... | collective-permute-start | bytes 1572872 | tf_op jit(solution)/shard_map/ppermute | solution.py:357
  51.5 17.7 %copy-start.9 = (bf16[256,2048]{1,0:T(8,128)(2,1)S(1)}, bf16[256,2048]{1,0:T(8,128)(2,1)}, u32[]{:S(2)}) copy-start(bf16[256,2048]{1,0:T(8,128)(2,1)} %copy-done.8) | copy-start | bytes 3145732
  66.5 14.8 %copy-start.6 = (bf16[256,2048]{1,0:T(8,128)(2,1)S(1)}, bf16[256,2048]{1,0:T(8,128)(2,1)}, u32[]{:S(2)}) copy-start(bf16[256,2048]{1,0:T(8,128)(2,1)} %param.31) | copy-start | bytes 3145732
  67.7 12.7 %collective-permute-start.3 = (bf16[128,2048]{1,0:T(8,128)(2,1)S(1)}, bf16[128,2048]{1,0:T(8,128)(2,1)S(1)}, u32[]{:S(2)}, u32[]{:S(2)}) collective-permute-start(bf16[128,2048]{1,0:T(8,128)(2,1)S(1)} %slice.317), channel_id=1, source_target_pairs={{0,1},{1,0},{2,3},{3,2},{4,5},{5,4},{6,7},{7,6},{8,9},{9,8},{10,11... | collective-permute-start | bytes 1572872 | tf_op jit(solution)/shard_map/ppermute | solution.py:357
  80.4 2.9 copy-start.14
  81.3 38.1 %collective-permute-start.14 = (bf16[256,2048]{1,0:T(8,128)(2,1)S(1)}, bf16[256,2048]{1,0:T(8,128)(2,1)S(1)}, u32[]{:S(2)}, u32[]{:S(2)}) collective-permute-start(bf16[256,2048]{1,0:T(8,128)(2,1)S(1)} %copy-done.6), channel_id=1, source_target_pairs={{0,1},{1,0},{2,3},{3,2},{4,5},{5,4},{6,7},{7,6},{8,9},{9,8},{10,11... | collective-permute-start | bytes 3145736 | tf_op jit(solution)/shard_map/ppermute | solution.py:357
  82.8 40.2 %collective-permute-start.15 = (bf16[256,2048]{1,0:T(8,128)(2,1)S(1)}, bf16[256,2048]{1,0:T(8,128)(2,1)S(1)}, u32[]{:S(2)}, u32[]{:S(2)}) collective-permute-start(bf16[256,2048]{1,0:T(8,128)(2,1)S(1)} %copy-done.6), channel_id=1, source_target_pairs={{0,2},{1,3},{2,0},{3,1},{4,6},{5,7},{6,4},{7,5},{8,10},{9,11},{10,... | collective-permute-start | bytes 3145736 | tf_op jit(solution)/shard_map/ppermute | solution.py:357
  114.3 1.3 copy-start.2
  115.6 9.3 %copy-start = (f32[1024,1024]{1,0:T(8,128)}, f32[1024,1024]{1,0:T(8,128)S(1)}, u32[]{:S(2)}) copy-start(f32[1024,1024]{1,0:T(8,128)S(1)} %get-tuple-element.24.y_ref) | copy-start | bytes 12582916
  115.6 17.2 %copy-start.1 = (f32[1024,1024]{1,0:T(8,128)}, f32[1024,1024]{1,0:T(8,128)S(1)}, u32[]{:S(2)}) copy-start(f32[1024,1024]{1,0:T(8,128)S(1)} %get-tuple-element.22.g_ref) | copy-start | bytes 12582916
  115.6 5.4 %collective-permute-start.8 = (f32[8,1024]{1,0:T(8,128)S(1)}, f32[8,1024]{1,0:T(8,128)S(1)}, u32[]{:S(2)}, u32[]{:S(2)}) collective-permute-start(f32[8,1024]{1,0:T(8,128)S(1)} %pad_maximum_fusion.10), channel_id=1, source_target_pairs={{0,2},{1,3},{2,0},{3,1},{4,6},{5,7},{6,4},{7,5},{8,10},{9,11},{10,... | collective-permute-start | bytes 98312 | tf_op jit(solution)/shard_map/ppermute | solution.py:357
  117.2 4.2 %collective-permute-start.7 = (f32[8,1024]{1,0:T(8,128)S(1)}, f32[8,1024]{1,0:T(8,128)S(1)}, u32[]{:S(2)}, u32[]{:S(2)}) collective-permute-start(f32[8,1024]{1,0:T(8,128)S(1)} %get-tuple-element.153), channel_id=1, source_target_pairs={{0,1},{1,0},{2,3},{3,2},{4,5},{5,4},{6,7},{7,6},{8,9},{9,8},{10,11... | collective-permute-start | bytes 98312 | tf_op jit(solution)/shard_map/ppermute | solution.py:357
  117.8 5.2 %collective-permute-start.9 = (f32[8,1024]{1,0:T(8,128)S(1)}, f32[8,1024]{1,0:T(8,128)S(1)}, u32[]{:S(2)}, u32[]{:S(2)}) collective-permute-start(f32[8,1024]{1,0:T(8,128)S(1)} %get-tuple-element.154), channel_id=1, source_target_pairs={{0,3},{1,2},{2,1},{3,0},{4,7},{5,6},{6,5},{7,4},{8,11},{9,10},{10,... | collective-permute-start | bytes 98312 | tf_op jit(solution)/shard_map/ppermute | solution.py:357
  119.4 11.1 %collective-permute-start.16 = (bf16[128,2048]{1,0:T(8,128)(2,1)S(1)}, bf16[128,2048]{1,0:T(8,128)(2,1)S(1)}, u32[]{:S(2)}, u32[]{:S(2)}) collective-permute-start(bf16[128,2048]{1,0:T(8,128)(2,1)S(1)} %slice.332), channel_id=1, source_target_pairs={{0,2},{1,3},{2,0},{3,1},{4,6},{5,7},{6,4},{7,5},{8,10},{9,11},{10,... | collective-permute-start | bytes 1572872 | tf_op jit(solution)/shard_map/ppermute | solution.py:357
  123.1 9.7 %collective-permute-start.17 = (bf16[128,2048]{1,0:T(8,128)(2,1)S(1)}, bf16[128,2048]{1,0:T(8,128)(2,1)S(1)}, u32[]{:S(2)}, u32[]{:S(2)}) collective-permute-start(bf16[128,2048]{1,0:T(8,128)(2,1)S(1)} %slice.333), channel_id=1, source_target_pairs={{0,1},{1,0},{2,3},{3,2},{4,5},{5,4},{6,7},{7,6},{8,9},{9,8},{10,11... | collective-permute-start | bytes 1572872 | tf_op jit(solution)/shard_map/ppermute | solution.py:357
  141.3 6.3 %copy-start.24 = (bf16[1024,1024]{1,0:T(8,128)(2,1)}, bf16[1024,1024]{1,0:T(8,128)(2,1)S(1)}, u32[]{:S(2)}) copy-start(bf16[1024,1024]{1,0:T(8,128)(2,1)S(1)} %get-tuple-element.112) | copy-start | bytes 6291460
  147.6 249.3 %reduce-scatter.4.cloned.1.call-start = ((), (), s32[]{:S(2)}) async-start(), calls=%async_computation.3 | async-start | bytes 4718592 | tf_op jit(solution)/shard_map/reduce_scatter | solution.py:493
  147.7 3.8 collective-permute-start.19
  148.5 3.7 collective-permute-start.18
  149.6 4.5 %collective-permute-start.20 = (f32[1024]{0:T(1024)S(1)}, f32[1024]{0:T(1024)S(1)}, u32[]{:S(2)}, u32[]{:S(2)}) collective-permute-start(f32[1024]{0:T(1024)S(1)} %get-tuple-element.162), channel_id=1, source_target_pairs={{0,3},{1,2},{2,1},{3,0},{4,7},{5,6},{6,5},{7,4},{8,11},{9,10},{10,... | collective-permute-start | bytes 12296 | tf_op jit(solution)/shard_map/ppermute | solution.py:357
  154.4 1.6 copy-start.3
  156.0 1.6 copy-start.4
  157.6 36.7 %copy-start.16 = (bf16[1024,2048]{1,0:T(8,128)(2,1)S(1)}, bf16[1024,2048]{1,0:T(8,128)(2,1)}, u32[]{:S(2)}) copy-start(bf16[1024,2048]{1,0:T(8,128)(2,1)} %constant_dynamic-update-slice_fusion) | copy-start | bytes 12582916
  202.1 1.6 copy-start.25
  202.1 197.0 %reduce-scatter.6.cloned.1.call-start = ((), (), s32[]{:S(2)}) async-start(), calls=%async_computation.4 | async-start | bytes 5308416 | tf_op jit(solution)/shard_map/reduce_scatter | solution.py:493
  203.7 7.1 %copy-start.19 = (bf16[1024,2048]{1,0:T(8,128)(2,1)S(1)}, bf16[1024,2048]{1,0:T(8,128)(2,1)}, u32[]{:S(2)}) copy-start(bf16[1024,2048]{1,0:T(8,128)(2,1)} %param.29) | copy-start | bytes 12582916
  208.3 103.2 %collective-permute-start.10 = (bf16[128,2048]{1,0:T(8,128)(2,1)}, bf16[128,2048]{1,0:T(8,128)(2,1)}, u32[]{:S(2)}, u32[]{:S(2)}) collective-permute-start(bf16[128,2048]{1,0:T(8,128)(2,1)} %get-tuple-element.129), channel_id=1, source_target_pairs={{0,2},{1,3},{2,0},{3,1},{4,6},{5,7},{6,4},{7,5},{8,10},{9,11},{10,... | collective-permute-start | bytes 1572872 | tf_op jit(solution)/shard_map/ppermute | solution.py:357
  210.0 104.8 %collective-permute-start.12 = (bf16[128,2048]{1,0:T(8,128)(2,1)}, bf16[128,2048]{1,0:T(8,128)(2,1)}, u32[]{:S(2)}, u32[]{:S(2)}) collective-permute-start(bf16[128,2048]{1,0:T(8,128)(2,1)} %get-tuple-element.130), channel_id=1, source_target_pairs={{0,1},{1,0},{2,3},{3,2},{4,5},{5,4},{6,7},{7,6},{8,9},{9,8},{10,11... | collective-permute-start | bytes 1572872 | tf_op jit(solution)/shard_map/ppermute | solution.py:357
  220.2 8.5 %collective-permute-start.25 = (bf16[1024,64]{1,0:T(8,128)(2,1)}, bf16[1024,64]{1,0:T(8,128)(2,1)S(1)}, u32[]{:S(2)}, u32[]{:S(2)}) collective-permute-start(bf16[1024,64]{1,0:T(8,128)(2,1)} %bitcast.25), channel_id=1, source_target_pairs={{0,1},{1,0},{2,3},{3,2},{4,5},{5,4},{6,7},{7,6},{8,9},{9,8},{10,11... | collective-permute-start | bytes 393224 | tf_op jit(solution)/shard_map/ppermute | solution.py:357
  222.3 9.5 %collective-permute-start.26 = (bf16[1024,64]{1,0:T(8,128)(2,1)}, bf16[1024,64]{1,0:T(8,128)(2,1)}, u32[]{:S(2)}, u32[]{:S(2)}) collective-permute-start(bf16[1024,64]{1,0:T(8,128)(2,1)} %bitcast.26), channel_id=1, source_target_pairs={{0,2},{1,3},{2,0},{3,1},{4,6},{5,7},{6,4},{7,5},{8,10},{9,11},{10,... | collective-permute-start | bytes 393224 | tf_op jit(solution)/shard_map/ppermute | solution.py:357
  223.5 8.3 %collective-permute-start.27 = (bf16[1024,64]{1,0:T(8,128)(2,1)}, bf16[1024,64]{1,0:T(8,128)(2,1)}, u32[]{:S(2)}, u32[]{:S(2)}) collective-permute-start(bf16[1024,64]{1,0:T(8,128)(2,1)} %bitcast.27), channel_id=1, source_target_pairs={{0,3},{1,2},{2,1},{3,0},{4,7},{5,6},{6,5},{7,4},{8,11},{9,10},{10,... | collective-permute-start | bytes 393224 | tf_op jit(solution)/shard_map/ppermute | solution.py:357
  246.3 35.0 %copy-start.15 = (bf16[128,2048]{1,0:T(8,128)(2,1)S(1)}, bf16[128,2048]{1,0:T(8,128)(2,1)}, u32[]{:S(2)}) copy-start(bf16[128,2048]{1,0:T(8,128)(2,1)} %copy-done.14) | copy-start | bytes 1572868
  281.3 12.8 %copy-start.10 = (bf16[256,2048]{1,0:T(8,128)(2,1)S(1)}, bf16[256,2048]{1,0:T(8,128)(2,1)}, u32[]{:S(2)}) copy-start(bf16[256,2048]{1,0:T(8,128)(2,1)} %copy-done.8) | copy-start | bytes 3145732
  289.5 19.4 %collective-permute-start.21 = (bf16[128,2048]{1,0:T(8,128)(2,1)S(1)}, bf16[128,2048]{1,0:T(8,128)(2,1)S(1)}, u32[]{:S(2)}, u32[]{:S(2)}) collective-permute-start(bf16[128,2048]{1,0:T(8,128)(2,1)S(1)} %get-tuple-element.123), channel_id=1, source_target_pairs={{0,2},{1,3},{2,0},{3,1},{4,6},{5,7},{6,4},{7,5},{8,10},{9,11},{10,... | collective-permute-start | bytes 1572872 | tf_op jit(solution)/shard_map/ppermute | solution.py:357
  290.6 19.7 %collective-permute-start.23 = (bf16[128,2048]{1,0:T(8,128)(2,1)}, bf16[128,2048]{1,0:T(8,128)(2,1)S(1)}, u32[]{:S(2)}, u32[]{:S(2)}) collective-permute-start(bf16[128,2048]{1,0:T(8,128)(2,1)} %get-tuple-element.124), channel_id=1, source_target_pairs={{0,1},{1,0},{2,3},{3,2},{4,5},{5,4},{6,7},{7,6},{8,9},{9,8},{10,11... | collective-permute-start | bytes 1572872 | tf_op jit(solution)/shard_map/ppermute | solution.py:357
  301.3 35.3 %slice-start = ((s8[9961472]{0:T(1024)(128)(4,1)}), s8[4194304]{0:T(1024)(128)(4,1)S(1)}, s32[]{:S(2)}) async-start(s8[9961472]{0:T(1024)(128)(4,1)} %bitcast.72), calls=%async_computation.6 | async-start | bytes 8388608
  301.3 35.3 %slice-start.1 = ((s8[9961472]{0:T(1024)(128)(4,1)}), s8[4194304]{0:T(1024)(128)(4,1)S(1)}, s32[]{:S(2)}) async-start(s8[9961472]{0:T(1024)(128)(4,1)} %bitcast.72), calls=%async_computation.7 | async-start | bytes 8388608
  308.9 2.5 copy-start.13
  309.1 26.2 %collective-permute-start.22 = (bf16[256,2048]{1,0:T(8,128)(2,1)S(1)}, bf16[256,2048]{1,0:T(8,128)(2,1)S(1)}, u32[]{:S(2)}, u32[]{:S(2)}) collective-permute-start(bf16[256,2048]{1,0:T(8,128)(2,1)S(1)} %pad_maximum_fusion.4), channel_id=1, source_target_pairs={{0,1},{1,0},{2,3},{3,2},{4,5},{5,4},{6,7},{7,6},{8,9},{9,8},{10,11... | collective-permute-start | bytes 3145736 | tf_op jit(solution)/shard_map/ppermute | solution.py:357
  310.3 4.5 %copy-start.12 = (bf16[256,2048]{1,0:T(8,128)(2,1)S(1)}, bf16[256,2048]{1,0:T(8,128)(2,1)}, u32[]{:S(2)}) copy-start(bf16[256,2048]{1,0:T(8,128)(2,1)} %convolution_convert_fusion.4) | copy-start | bytes 3145732
  310.3 26.4 %slice-start.2 = ((s8[9961472]{0:T(1024)(128)(4,1)}), s8[1572864]{0:T(1024)(128)(4,1)S(1)}, s32[]{:S(2)}) async-start(s8[9961472]{0:T(1024)(128)(4,1)} %bitcast.72), calls=%async_computation.8 | async-start | bytes 3145728
  310.5 26.2 %copy-start.5 = (bf16[256,2048]{1,0:T(8,128)(2,1)S(1)}, bf16[256,2048]{1,0:T(8,128)(2,1)}, u32[]{:S(2)}) copy-start(bf16[256,2048]{1,0:T(8,128)(2,1)} %param.16) | copy-start | bytes 3145732
  310.5 26.2 %copy-start.17 = (f32[2048]{0:T(1024)S(1)}, f32[2048]{0:T(1024)}, u32[]{:S(2)}) copy-start(f32[2048]{0:T(1024)} %param.17) | copy-start | bytes 24580
  310.5 26.2 %collective-permute-start.24 = (bf16[256,2048]{1,0:T(8,128)(2,1)S(1)}, bf16[256,2048]{1,0:T(8,128)(2,1)S(1)}, u32[]{:S(2)}, u32[]{:S(2)}) collective-permute-start(bf16[256,2048]{1,0:T(8,128)(2,1)S(1)} %pad_maximum_fusion.5), channel_id=1, source_target_pairs={{0,2},{1,3},{2,0},{3,1},{4,6},{5,7},{6,4},{7,5},{8,10},{9,11},{10,... | collective-permute-start | bytes 3145736 | tf_op jit(solution)/shard_map/ppermute | solution.py:357
  313.7 74.5 %collective-permute-start.11 = (bf16[256,2048]{1,0:T(8,128)(2,1)}, bf16[256,2048]{1,0:T(8,128)(2,1)}, u32[]{:S(2)}, u32[]{:S(2)}) collective-permute-start(bf16[256,2048]{1,0:T(8,128)(2,1)} %pad_maximum_fusion.2), channel_id=1, source_target_pairs={{0,1},{1,0},{2,3},{3,2},{4,5},{5,4},{6,7},{7,6},{8,9},{9,8},{10,11... | collective-permute-start | bytes 3145736 | tf_op jit(solution)/shard_map/ppermute | solution.py:357
  317.0 71.2 %copy-start.7 = (bf16[256,2048]{1,0:T(8,128)(2,1)S(1)}, bf16[256,2048]{1,0:T(8,128)(2,1)}, u32[]{:S(2)}) copy-start(bf16[256,2048]{1,0:T(8,128)(2,1)} %param.31) | copy-start | bytes 3145732
  317.0 71.2 %collective-permute-start.13 = (bf16[256,2048]{1,0:T(8,128)(2,1)}, bf16[256,2048]{1,0:T(8,128)(2,1)}, u32[]{:S(2)}, u32[]{:S(2)}) collective-permute-start(bf16[256,2048]{1,0:T(8,128)(2,1)} %pad_maximum_fusion.3), channel_id=1, source_target_pairs={{0,2},{1,3},{2,0},{3,1},{4,6},{5,7},{6,4},{7,5},{8,10},{9,11},{10,... | collective-permute-start | bytes 3145736 | tf_op jit(solution)/shard_map/ppermute | solution.py:357
  336.7 6.4 %copy-start.11 = (bf16[256,2048]{1,0:T(8,128)(2,1)}, bf16[256,2048]{1,0:T(8,128)(2,1)S(1)}, u32[]{:S(2)}) copy-start(bf16[256,2048]{1,0:T(8,128)(2,1)S(1)} %collective-permute-done.24) | copy-start | bytes 3145732
Sparse Core Ops, SparseCore 0:
  147.7 50.1 reduce-scatter.7
  202.2 50.6 reduce-scatter.3
  255.2 53.3 reduce-scatter.5
